TPU v7x, 32 devices: a whole 2x2x4 slice. The times are simulated.
32 devices in a mesh: row: 2 (over x), col: 16 (over z, y, core).
Axes of the slice: x: 2, y: 2, z: 4, core: 2. Of those that a mesh axis runs over, the one named last changes fastest.
Arguments:
- a_blocks: bfloat16 [512, 7, 64, 64], P(('row', 'col')), may hold values from -1.796875 to 1.796875
- p_blocks: bfloat16 [512, 64, 64], P(('row', 'col')), may hold values from -0.75 to 0.75
- a_peer: int32 [512, 7], P(('row', 'col')), may hold values from 0 to 15, all different within a row; in each aligned block of 16 rows (0 to 15, 16 to 31, ...) at most 8 rows name the same one
- a_local: int32 [512, 7], P(('row', 'col')), may hold values from 0 to 15
- agg_owner: int32 [512, 1], P(('row', 'col')), may hold values from 0 to 1; in each aligned block of 16 rows (0 to 15, 16 to 31, ...) at most 9 rows name the same one
- agg_local: int32 [512], P(('row', 'col')), may hold values from 0 to 3
- entry_slot: int32 [512, 7], P(('row', 'col')), may hold values from 0 to 6
Outputs:
- coarse: bfloat16 [128, 7, 64, 64], P(('row', 'col'))
Inputs may be any that keep to these rules, and one draw needn't show every extreme that they name: `a_peer`: each fine block row names 7 different devices; among the rows of one device no device is named more than 8 times, and some device is named exactly that often. `agg_owner`: among the rows of one device no region is named more than 9 times, and some region is named exactly that often.
All inputs are finite; a program needn't handle non-finite values.
Results may differ from a plain program's by a relative error of at most 0.0049.
Values may be sent and summed in bfloat16 or wider, within the bound.
No kernel may reach another device: no remote copies, remote signals or barrier semaphores. Data moves between devices by JAX's collectives and lax.ppermute only.
A program may use at most 64 MiB of HBM per device.

v0:
```python
import jax
import jax.numpy as jnp
from jax import lax
from jax.sharding import PartitionSpec as P

KC = 7
NC_DEV = 4


def slot_ranks(targets, target_count):
    matches = (targets[:, None] == jnp.arange(target_count, dtype=jnp.int32)[None, :]).astype(
        jnp.int32
    )
    return jnp.sum((jnp.cumsum(matches, axis=0) - 1) * matches, axis=1)


def local(a_blocks, p_blocks, a_peer, a_local, agg_owner, agg_local, entry_slot):
    block_rows, entry_count, block_order, _ = a_blocks.shape
    columns = lax.axis_size("col")
    regions = lax.axis_size("row")
    capacity = (block_rows * entry_count + columns - 1) // columns + 1
    flat_peer = a_peer.reshape(-1)
    flat_local = a_local.reshape(-1)
    peer_rank = slot_ranks(flat_peer, columns)
    wanted = jnp.zeros((columns, capacity), jnp.int32).at[flat_peer, peer_rank].set(flat_local)
    served = p_blocks[lax.all_to_all(wanted, "col", split_axis=0, concat_axis=0, tiled=True)]
    returned = lax.all_to_all(served, "col", split_axis=0, concat_axis=0, tiled=True)
    fetched = returned[flat_peer, peer_rank].reshape(a_blocks.shape)
    product_ap = jnp.einsum(
        "nkab,nkbc->nkac", a_blocks, fetched, preferred_element_type=jnp.float32
    ).astype(jnp.bfloat16)
    coarse_lanes = NC_DEV * KC
    local_target = agg_local[:, None] * KC + entry_slot
    owners = agg_owner[:, 0]
    terms = jnp.einsum("nba,nkbc->nkac", p_blocks, product_ap, preferred_element_type=jnp.float32)
    full_target = (owners[:, None] * coarse_lanes + local_target).reshape(-1)
    lane_total = regions * coarse_lanes
    one_hot = (full_target[None, :] == jnp.arange(lane_total, dtype=jnp.int32)[:, None]).astype(
        jnp.float32
    )
    partial_value = jnp.dot(
        one_hot,
        terms.reshape(block_rows * entry_count, block_order * block_order),
        precision=lax.Precision.HIGHEST,
    )
    summed = lax.psum_scatter(partial_value, "row", scatter_dimension=0, tiled=True)
    return summed.reshape(NC_DEV, KC, block_order, block_order).astype(jnp.bfloat16)


def solution(mesh):
    in_specs = (
        P(("row", "col"), None, None, None),
        P(("row", "col"), None, None),
        P(("row", "col"), None),
        P(("row", "col"), None),
        P(("row", "col"), None),
        P(("row", "col")),
        P(("row", "col"), None),
    )
    out_specs = P(("row", "col"), None, None, None)
    return jax.shard_map(local, mesh=mesh, in_specs=in_specs, out_specs=out_specs, check_vma=False)
```

profile of v0, /device:TPU:0, one launch (start us, length us, event | category | flops | bytes accessed | tf_op | source)
XLA Modules:
  0.0 101.8 jit_solution(14405939806295972307)
XLA Ops:
  0.0 0.0 copy-start
  0.0 0.0 copy-start.1
  0.0 0.9 copy.20
  0.9 0.1 eq.34
  1.0 0.1 reshape.89
  1.1 0.1 fusion.6
  1.2 0.2 reduce_window_sum.11
  1.3 0.2 select_reduce_fusion
  1.5 0.8 copy.22
  2.3 0.1 reshape.109
  2.4 5.7 %scatter_fusion = s32[16,8]{0,1:T(8,128)S(1)} fusion(s32[16,8]{0,1:T(8,128)S(1)} %broadcast.72, s32[112]{0:T(128)S(1)} %get-tuple-element.5, s32[112]{0:T(128)S(1)} %reshape.109), kind=kCustom, calls=%fused_computation.2 | custom fusion | bytes 2240 | tf_op jit(solution)/shard_map/scatter | solution.py:25
  8.1 0.1 copy.23
  8.2 13.6 %all_to_all.17 = s32[16,1,8]{2,1,0:T(1,128)S(1)} all-to-all(s32[16,1,8]{2,1,0:T(1,128)S(1)} %copy.23), channel_id=1, replica_groups=mesh['row'=2,'col'=16] {'col'}, dimensions={0} | all-to-all | bytes 1024 | tf_op jit(solution)/shard_map/all_to_all | solution.py:26
  21.8 0.1 copy.24
  21.9 0.1 copy.25
  22.0 0.1 reshape.95
  22.1 0.0 copy-done.1
  22.1 2.2 %gather_fusion = bf16[128,64,64]{2,1,0:T(8,128)(2,1)} fusion(bf16[16,64,64]{2,1,0:T(8,128)(2,1)S(1)} %copy-done.1, s32[1024]{0:T(1024)S(1)} %pad_clamp_fusion), kind=kCustom, calls=%fused_computation | custom fusion | bytes 2097664 | tf_op jit(solution)/shard_map/gather | solution.py:26
  24.3 0.0 copy-start.4
  24.3 4.6 %reshape.116 = bf16[16,2,16384]{2,1,0:T(2,128)(2,1)} reshape(bf16[16,8,64,64]{3,2,1,0:T(8,128)(2,1)} %bitcast.39) | data formatting | bytes 2097152
  28.9 0.0 copy-start.5
  28.9 0.0 copy-start.2
  28.9 3.8 %all-to-all-start.1 = ((bf16[16,2,16384]{2,1,0:T(2,128)(2,1)}), bf16[16,2,16384]{2,1,0:T(2,128)(2,1)S(1)}, u32[]{:S(2)}, u32[]{:S(2)}) async-start(bf16[16,2,16384]{2,1,0:T(2,128)(2,1)} %reshape.116), calls=%async_computation.1 | async-start | bytes 2097152 | tf_op jit(solution)/shard_map/all_to_all | solution.py:27
  32.7 0.0 copy-done.4
  32.7 0.0 copy-done.5
  32.7 0.0 copy-done.2
  32.8 0.1 copy.19
  32.8 0.1 eq.30
  32.9 22.6 %all-to-all-done.1 = bf16[16,2,16384]{2,1,0:T(2,128)(2,1)S(1)} async-done(((bf16[16,2,16384]{2,1,0:T(2,128)(2,1)}), bf16[16,2,16384]{2,1,0:T(2,128)(2,1)S(1)}, u32[]{:S(2)}, u32[]{:S(2)}) %all-to-all-start.1) | async-done | bytes 1048608 | tf_op jit(solution)/shard_map/all_to_all | solution.py:27
  55.5 2.4 %reshape.117 = bf16[16,8,64,64]{3,2,1,0:T(8,128)(2,1)} reshape(bf16[16,2,16384]{2,1,0:T(2,128)(2,1)S(1)} %all-to-all-done.1) | data formatting | bytes 2097152
  57.9 4.1 %gather_fusion.1 = bf16[112,64,64]{2,1,0:T(8,128)(2,1)} fusion(bf16[16,8,64,64]{3,2,1,0:T(8,128)(2,1)} %reshape.117, s32[112]{0:T(128)S(1)} %bitcast.41), kind=kCustom, calls=%fused_computation.1 | custom fusion | bytes 1835904 | tf_op jit(solution)/shard_map/gather | solution.py:28
  62.0 0.0 copy-done
  62.0 4.9 %convolution_bitcast_fusion = f32[16,7,64,64]{2,3,1,0:T(8,128)} fusion(bf16[16,7,64,64]{3,2,1,0:T(8,128)(2,1)} %bitcast.40, bf16[16,7,64,64]{3,2,1,0:T(8,128)(2,1)S(1)} %copy-done, bf16[16,64,64]{2,1,0:T(8,128)(2,1)S(1)} %copy-done.1), kind=kOutput, calls=%fused_computation.3 | convolution fusion | flops 117899264 | bytes 3801088 | tf_op jit(solution)/shard_map/nba,nkbc->nkac/dot_general | solution.py:35
  66.9 5.0 %copy.27 = f32[16,7,64,64]{3,2,1,0:T(8,128)} copy(f32[16,7,64,64]{2,3,1,0:T(8,128)} %convolution_bitcast_fusion) | data formatting | bytes 3670016 | tf_op jit(solution)/shard_map/nba,nkbc->nkac/transpose | solution.py:35
  71.9 4.1 %reshape.92 = f32[112,4096]{1,0:T(8,128)} reshape(f32[16,7,64,64]{3,2,1,0:T(8,128)} %copy.27) | data formatting | bytes 3670016 | tf_op jit(solution)/shard_map/reshape | solution.py:43
  76.0 0.0 copy-start.3
  76.0 2.3 %fusion.7 = f32[56,4096]{1,0:T(8,128)S(1)} fusion(f32[112,4096]{1,0:T(8,128)} %reshape.92, s32[112]{0:T(128)S(1)} %eq.30), kind=kOutput, calls=%fused_computation.13 | convolution fusion | flops 308287616 | bytes 2752960 | tf_op jit(solution)/shard_map/dot_general | solution.py:41
  78.3 17.6 %fusion = f32[32,4096]{1,0:T(8,128)S(1)} fusion(f32[56,4096]{1,0:T(8,128)S(1)} %fusion.7), kind=kCustom, calls=%all-reduce-scatter | all-reduce-scatter fusion | flops 262145 | bytes 1442304
  96.0 2.4 %collective-permute-start = (bf16[4,4096]{1,0:T(4,128)(2,1)S(1)}, bf16[4,4096]{1,0:T(4,128)(2,1)S(1)}, u32[]{:S(2)}, u32[]{:S(2)}) collective-permute-start(bf16[4,4096]{1,0:T(4,128)(2,1)S(1)} %slice.6), channel_id=1, source_target_pairs={{0,16},{1,17},{2,18},{3,19},{4,20},{5,21},{6,22},{7,23},{8,24},{9,... | collective-permute-start | bytes 98312
  98.4 0.0 copy-done.3
  98.4 0.6 dynamic-slice.4
  99.7 0.3 collective-permute-done
  100.0 0.5 concatenate.9
  100.5 0.1 dynamic-slice_convert_fusion
  100.6 1.2 %convert_element_type.20 = bf16[4,7,64,64]{3,2,1,0:T(8,128)(2,1)} reshape(bf16[28,4096]{1,0:T(8,128)(2,1)S(1)} %dynamic-slice_convert_fusion) | data formatting | bytes 458752 | tf_op jit(solution)/shard_map/convert_element_type | solution.py:47
  (8 shorter events, 0.1 us)
Async XLA Ops:
  0.0 62.0 %copy-start = (bf16[16,7,64,64]{3,2,1,0:T(8,128)(2,1)S(1)}, bf16[16,7,64,64]{3,2,1,0:T(8,128)(2,1)}, u32[]{:S(2)}) copy-start(bf16[16,7,64,64]{3,2,1,0:T(8,128)(2,1)} %param.7) | copy-start | bytes 2752516
  0.0 22.1 %copy-start.1 = (bf16[16,64,64]{2,1,0:T(8,128)(2,1)S(1)}, bf16[16,64,64]{2,1,0:T(8,128)(2,1)}, u32[]{:S(2)}) copy-start(bf16[16,64,64]{2,1,0:T(8,128)(2,1)} %param.8) | copy-start | bytes 393220
  24.3 8.4 %copy-start.4 = (s32[16]{0:T(128)S(1)}, s32[16]{0:T(128)}, u32[]{:S(2)}) copy-start(s32[16]{0:T(128)} %param.12) | copy-start | bytes 196
  28.9 3.8 %copy-start.5 = (s32[16,1]{0,1:T(1,128)S(1)}, s32[16,1]{0,1:T(1,128)}, u32[]{:S(2)}) copy-start(s32[16,1]{0,1:T(1,128)} %param.11) | copy-start | bytes 196
  28.9 3.8 %copy-start.2 = (s32[16,7]{0,1:T(8,128)S(1)}, s32[16,7]{0,1:T(8,128)}, u32[]{:S(2)}) copy-start(s32[16,7]{0,1:T(8,128)} %param.13) | copy-start | bytes 1348
  28.9 26.6 %all-to-all-start.1 = ((bf16[16,2,16384]{2,1,0:T(2,128)(2,1)}), bf16[16,2,16384]{2,1,0:T(2,128)(2,1)S(1)}, u32[]{:S(2)}, u32[]{:S(2)}) async-start(bf16[16,2,16384]{2,1,0:T(2,128)(2,1)} %reshape.116), calls=%async_computation.1 | async-start | bytes 2097152 | tf_op jit(solution)/shard_map/all_to_all | solution.py:27
  76.0 22.4 %copy-start.3 = (u32[32]{0:T(128)S(1)}, u32[32]{0:T(128)}, u32[]{:S(2)}) copy-start(u32[32]{0:T(128)} %constant.58) | copy-start | bytes 388
  96.0 4.0 %collective-permute-start = (bf16[4,4096]{1,0:T(4,128)(2,1)S(1)}, bf16[4,4096]{1,0:T(4,128)(2,1)S(1)}, u32[]{:S(2)}, u32[]{:S(2)}) collective-permute-start(bf16[4,4096]{1,0:T(4,128)(2,1)S(1)} %slice.6), channel_id=1, source_target_pairs={{0,16},{1,17},{2,18},{3,19},{4,20},{5,21},{6,22},{7,23},{8,24},{9,... | collective-permute-start | bytes 98312
where the time goes:
time: 104 us; the launch traced here: 102 us
  local copies, waits for them, and re-layouts  32.9 us (32%)
  blocking collectives  31.2 us (30%)
  waiting for transfers between devices  22.9 us (22%)
  matrix products  7.21 us (7%)
  starting transfers between devices  6.23 us (6%)
    all_to_all x1, waiting for transfers between devices, local(): lax.all_to_all(served, 'col', split_axis=0, concat_axis=0, tiled=True)  22.6 us
    unnamed x1, blocking collectives  17.6 us
    all_to_all x1, blocking collectives, local(): lax.all_to_all(wanted, 'col', split_axis=0, concat_axis=0, tiled=True)  13.6 us
    unnamed x19, local copies, waits for them, and re-layouts  9.79 us
    scatter x1, local copies, waits for them, and re-layouts, local(): jnp.zeros((columns, capacity), jnp.int32).at[flat_peer, peer_rank]  5.7 us
    transpose x1, local copies, waits for them, and re-layouts, local(): jnp.einsum('nba,nkbc->nkac', p_blocks, product_ap, preferred_element_type...  4.99 us
    dot_general x1, matrix products, local(): jnp.einsum('nba,nkbc->nkac', p_blocks, product_ap, preferred_element_type...  4.91 us
    reshape x1, local copies, waits for them, and re-layouts, local(): terms.reshape(block_rows * entry_count, block_order * block_order)  4.14 us
  transfers between devices with their start and end apart: 2, of which 2 were waited for; matrix products, arithmetic and copies ran while one was open for 1% of the time, Pallas kernels for 0%

commit v1 on v0

v1 whole, which is shorter than its diff:
```python
import jax
import jax.numpy as jnp
from jax import lax
from jax.experimental import pallas as pl
from jax.experimental.pallas import tpu as pltpu
from jax.sharding import PartitionSpec as P

KC = 7
NC_DEV = 4
VMEM = pl.BlockSpec(memory_space=pltpu.VMEM)
SMEM = pl.BlockSpec(memory_space=pltpu.SMEM)


def ring_position(index, chips):
    z, y = index // 4, index // 2 % 2
    return z + y * (chips - 1 - 2 * z)


def pack_kernel(p_ref, out_ref):
    pairs, order, _ = out_ref.shape
    for j in range(pairs):
        out_ref[j] = jnp.concatenate([p_ref[j], p_ref[j + pairs]], axis=1)


def left_kernel(a_ref, p_ref, x_ref):
    rows, entries = a_ref.shape[:2]
    for i in range(rows):
        for k in range(entries):
            x = lax.dot_general(
                p_ref[i], a_ref[i, k], (((0,), (0,)), ((), ())), preferred_element_type=jnp.float32
            )
            x_ref[i * entries + k] = x.astype(x_ref.dtype)


def fold(acc_ref, base, half, j, low):
    rows = acc_ref.shape[0] // 2
    first = jnp.where(low, acc_ref[base + j], acc_ref[rows + base + half + j])
    second = jnp.where(low, acc_ref[base + half + j], acc_ref[rows + base + j])
    order = first.shape[1] // 2
    return first + pltpu.roll(second, order, axis=1)


def sum_kernel(code_ref, x_ref, *refs):
    *pieces, own_ref, sent_ref, gathered_ref, acc_ref = refs
    entries, rows = code_ref.shape
    pairs, order, width = pieces[0].shape
    acc_ref[...] = jnp.zeros_like(acc_ref)
    for n, piece in enumerate(pieces):
        gathered_ref[n * pairs : (n + 1) * pairs] = piece[...]
    for i in range(rows):
        for k in range(entries):
            code = code_ref[k, i]
            source, target = code >> 16, code & 0xFFFF
            acc_ref[target] += jnp.dot(
                x_ref[i * entries + k], gathered_ref[source], preferred_element_type=jnp.float32
            )
    lanes = lax.broadcasted_iota(jnp.int32, (order, width), 1)
    low = lanes < width // 2
    half = own_ref.shape[0]
    for j in range(half):
        own_ref[j] = fold(acc_ref, 0, half, j, low)
    for n in range(sent_ref.shape[0]):
        for j in range(half):
            sent_ref[n, j] = fold(acc_ref, 2 * half * (n + 1), half, j, low).astype(sent_ref.dtype)


def add_kernel(own_ref, *refs):
    *received, out_ref = refs
    half, order, width = own_ref.shape
    for j in range(half):
        total = own_ref[j]
        for ref in received:
            total = total + ref[j].astype(jnp.float32)
        total = total.astype(out_ref.dtype)
        out_ref[j] = total[:, : width // 2]
        out_ref[half + j] = total[:, width // 2 :]


def local(a_blocks, p_blocks, a_peer, a_local, agg_owner, agg_local, entry_slot):
    rows, entries, order, _ = a_blocks.shape
    columns, regions = lax.axis_size("col"), lax.axis_size("row")
    chips = columns // 2
    pairs = rows // 2
    lanes = NC_DEV * KC

    def toward(index, step):
        place = (ring_position(index, chips) + step) % chips
        z, y = (place, 0) if place < chips // 2 else (chips - 1 - place, 1)
        return z * 4 + y * 2 + index % 2

    ring = [(i, toward(i, 1 - 2 * (i % 2))) for i in range(columns)]
    swap = [(i, i ^ 1) for i in range(columns)]

    own = pl.pallas_call(
        pack_kernel,
        out_shape=jax.ShapeDtypeStruct((pairs, order, 2 * order), p_blocks.dtype),
        in_specs=[VMEM], out_specs=VMEM, name="pack",
    )(p_blocks)

    first, second = own, lax.ppermute(own, "col", swap)
    behind, ahead = {0: (own, second)}, {}
    for step in range(1, chips // 2 + 1):
        first = lax.ppermute(first, "col", ring)
        if step < chips // 2:
            second = lax.ppermute(second, "col", ring)
            behind[step] = (first, second)
            ahead[step] = (lax.ppermute(second, "col", swap), lax.ppermute(first, "col", swap))
        else:
            ahead[step] = (first, lax.ppermute(first, "col", swap))
    pieces = []
    for distance in range(chips):
        if distance == 0:
            pieces += behind[0]
        elif distance <= chips // 2:
            pieces += ahead[distance]
        else:
            pieces += behind[chips - distance]

    x = pl.pallas_call(
        left_kernel,
        out_shape=jax.ShapeDtypeStruct((rows * entries, order, order), jnp.bfloat16),
        in_specs=[VMEM, VMEM], out_specs=VMEM, name="left",
    )(a_blocks, p_blocks)

    me, region = lax.axis_index("col"), lax.axis_index("row")
    peer, place = a_peer.T, a_local.T
    turned = me % 2
    distance = ring_position(peer, chips) - ring_position(me, chips)
    distance = (distance * (1 - 2 * turned)) % chips
    source = (distance * 2 + (peer % 2) ^ turned) * pairs + place % pairs
    relative = (agg_owner.T - region) % regions
    target = relative * lanes + agg_local[None, :] * KC + entry_slot.T
    code = source * 65536 + target + (place // pairs) * (regions * lanes)

    half = lanes // 2
    width = 2 * order
    own_sum, sent = pl.pallas_call(
        sum_kernel,
        out_shape=(
            jax.ShapeDtypeStruct((half, order, width), jnp.float32),
            jax.ShapeDtypeStruct((regions - 1, half, order, width), jnp.bfloat16),
        ),
        in_specs=[SMEM] + [VMEM] * (1 + len(pieces)), out_specs=(VMEM, VMEM),
        scratch_shapes=[
            pltpu.VMEM((columns * pairs, order, width), p_blocks.dtype),
            pltpu.VMEM((2 * regions * lanes, order, width), jnp.float32),
        ],
        name="sum",
    )(code, x, *pieces)

    received = [
        lax.ppermute(sent[n - 1], "row", [(i, (i + n) % regions) for i in range(regions)])
        for n in range(1, regions)
    ]
    out = pl.pallas_call(
        add_kernel,
        out_shape=jax.ShapeDtypeStruct((lanes, order, order), jnp.bfloat16),
        in_specs=[VMEM] * regions, out_specs=VMEM, name="add",
    )(own_sum, *received)
    return out.reshape(NC_DEV, KC, order, order)


def solution(mesh):
    in_specs = (
        P(("row", "col"), None, None, None),
        P(("row", "col"), None, None),
        P(("row", "col"), None),
        P(("row", "col"), None),
        P(("row", "col"), None),
        P(("row", "col")),
        P(("row", "col"), None),
    )
    out_specs = P(("row", "col"), None, None, None)
    return jax.shard_map(local, mesh=mesh, in_specs=in_specs, out_specs=out_specs, check_vma=False)
```

time: 104 us -> 44.7 us (0.43); the launches traced: 102 us -> 44.5 us
  local copies, waits for them, and re-layouts: 32.9 us -> 1.45 us
  blocking collectives: 31.2 us -> 0 us
  Pallas kernels: 0 us -> 11.6 us
  starting transfers between devices: 6.23 us -> 16.1 us
  waiting for transfers between devices: 22.9 us -> 14.5 us
  matrix products: 7.21 us -> 0 us
    all_to_all x1 -> x0, waiting for transfers between devices: 22.6 us -> none  [local(): lax.all_to_all(served, 'col', split_axis=0, concat_axis=0, tiled=True)]
    unnamed x1 -> x0, blocking collectives: 17.6 us -> none
    ppermute x0 -> x16, starting transfers between devices: none -> 16.1 us  [the longest x4 8.79 us: local(): first = lax.ppermute(first, 'col', ring)]
    ppermute x0 -> x16, waiting for transfers between devices: none -> 14.5 us  [the longest x1 6.7 us: local(): lax.ppermute(sent[n - 1], 'row', [(i, (i + n) % regions) for i in range(r...]
    all_to_all x1 -> x0, blocking collectives: 13.6 us -> none  [local(): lax.all_to_all(wanted, 'col', split_axis=0, concat_axis=0, tiled=True)]
    pallas_call x0 -> x4, Pallas kernels: none -> 11.6 us  [the longest x1 4.38 us: local(): pl.pallas_call(sum_kernel, out_shape=(jax.ShapeDtypeStruct((half, order,...]
    unnamed x19 -> x42, local copies, waits for them, and re-layouts: 9.79 us -> 1.45 us
    dot_general x2 -> x0, matrix products: 7.21 us -> none  [the longest x1 4.91 us: local(): jnp.einsum('nba,nkbc->nkac', p_blocks, product_ap, preferred_element_type...]
  transfers between devices with their start and end apart: 2 -> 16, of which waited for: 2 -> 6; matrix products, arithmetic and copies ran while one was open for 1% -> 1% of each run, Pallas kernels for 0% -> 8%
where the time goes in v1:
time: 44.7 us; the launch traced here: 44.5 us
  starting transfers between devices  16.1 us (36%)
  waiting for transfers between devices  14.5 us (32%)
  Pallas kernels  11.6 us (26%)
  local copies, waits for them, and re-layouts  1.45 us (3%)
  other arithmetic  0.64 us (1%)
    ppermute x4, starting transfers between devices, local(): first = lax.ppermute(first, 'col', ring)  8.79 us
    ppermute x1, waiting for transfers between devices, local(): lax.ppermute(sent[n - 1], 'row', [(i, (i + n) % regions) for i in range(r...  6.7 us
    ppermute x4, waiting for transfers between devices, local(): first = lax.ppermute(first, 'col', ring)  5.56 us
    ppermute x3, starting transfers between devices, local(): second = lax.ppermute(second, 'col', ring)  4.67 us
    pallas_call x1, Pallas kernels, local(): pl.pallas_call(sum_kernel, out_shape=(jax.ShapeDtypeStruct((half, order,...  4.38 us
    pallas_call x1, Pallas kernels, local(): pl.pallas_call(left_kernel, out_shape=jax.ShapeDtypeStruct((rows * entrie...  3.49 us
    pallas_call x1, Pallas kernels, local(): pl.pallas_call(add_kernel, out_shape=jax.ShapeDtypeStruct((lanes, order,...  2.03 us
    pallas_call x1, Pallas kernels, local(): pl.pallas_call(pack_kernel, out_shape=jax.ShapeDtypeStruct((pairs, order,...  1.7 us
  transfers between devices with their start and end apart: 16, of which 6 were waited for; matrix products, arithmetic and copies ran while one was open for 1% of the time, Pallas kernels for 8%

profile of v1, /device:TPU:0, one launch (start us, length us, event | category | flops | bytes accessed | tf_op | source)
XLA Modules:
  0.0 44.5 jit_solution(11712984623475628100)
XLA Ops:
  0.0 1.7 %pack.1.refs_0_ = bf16[8,64,128]{2,1,0:T(8,128)(2,1)} custom-call(bf16[16,64,64]{2,1,0:T(8,128)(2,1)} %p_ref.3), custom_call_target="tpu_custom_call" | custom-call | tf_op jit(solution)/shard_map/pack/pallas_call | solution.py:94
  1.7 3.1 %collective-permute-start.3 = (bf16[8,64,128]{2,1,0:T(8,128)(2,1)}, bf16[8,64,128]{2,1,0:T(8,128)(2,1)S(1)}, u32[]{:S(2)}, u32[]{:S(2)}) collective-permute-start(bf16[8,64,128]{2,1,0:T(8,128)(2,1)} %pack.1.refs_0_), channel_id=1, source_target_pairs={{0,4},{1,3},{2,0},{3,7},{4,8},{5,1},{6,2},{7,11},{8,12},{9,5},{10,... | collective-permute-start | bytes 393224 | tf_op jit(solution)/shard_map/ppermute | solution.py:103
  4.8 0.0 collective-permute-start
  4.8 3.1 %collective-permute-done.3.refs_14_ = bf16[8,64,128]{2,1,0:T(8,128)(2,1)S(1)} collective-permute-done((bf16[8,64,128]{2,1,0:T(8,128)(2,1)}, bf16[8,64,128]{2,1,0:T(8,128)(2,1)S(1)}, u32[]{:S(2)}, u32[]{:S(2)}) %collective-permute-start.3) | collective-permute-done | bytes 131104 | tf_op jit(solution)/shard_map/ppermute | solution.py:103
  7.9 2.1 %collective-permute-start.7 = (bf16[8,64,128]{2,1,0:T(8,128)(2,1)S(1)}, bf16[8,64,128]{2,1,0:T(8,128)(2,1)S(1)}, u32[]{:S(2)}, u32[]{:S(2)}) collective-permute-start(bf16[8,64,128]{2,1,0:T(8,128)(2,1)S(1)} %collective-permute-done.3.refs_14_), channel_id=1, source_target_pairs={{0,4},{1,3},{2,0},{3,7},{4,8},{5,1},{6,2},{7,11},{8,12},{9,5},{10,... | collective-permute-start | bytes 393224 | tf_op jit(solution)/shard_map/ppermute | solution.py:103
  9.9 0.0 collective-permute-done.refs_1_
  9.9 1.6 %collective-permute-start.1 = (bf16[8,64,128]{2,1,0:T(8,128)(2,1)S(1)}, bf16[8,64,128]{2,1,0:T(8,128)(2,1)S(1)}, u32[]{:S(2)}, u32[]{:S(2)}) collective-permute-start(bf16[8,64,128]{2,1,0:T(8,128)(2,1)S(1)} %collective-permute-done.refs_1_), channel_id=1, source_target_pairs={{0,4},{1,3},{2,0},{3,7},{4,8},{5,1},{6,2},{7,11},{8,12},{9,5},{10,... | collective-permute-start | bytes 393224 | tf_op jit(solution)/shard_map/ppermute | solution.py:105
  11.5 1.3 %collective-permute-done.7.refs_12_ = bf16[8,64,128]{2,1,0:T(8,128)(2,1)S(1)} collective-permute-done((bf16[8,64,128]{2,1,0:T(8,128)(2,1)S(1)}, bf16[8,64,128]{2,1,0:T(8,128)(2,1)S(1)}, u32[]{:S(2)}, u32[]{:S(2)}) %collective-permute-start.7) | collective-permute-done | bytes 131104 | tf_op jit(solution)/shard_map/ppermute | solution.py:103
  12.8 2.1 %collective-permute-start.11 = (bf16[8,64,128]{2,1,0:T(8,128)(2,1)S(1)}, bf16[8,64,128]{2,1,0:T(8,128)(2,1)S(1)}, u32[]{:S(2)}, u32[]{:S(2)}) collective-permute-start(bf16[8,64,128]{2,1,0:T(8,128)(2,1)S(1)} %collective-permute-done.7.refs_12_), channel_id=1, source_target_pairs={{0,4},{1,3},{2,0},{3,7},{4,8},{5,1},{6,2},{7,11},{8,12},{9,5},{10,... | collective-permute-start | bytes 393224 | tf_op jit(solution)/shard_map/ppermute | solution.py:103
  14.9 0.0 collective-permute-done.1.refs_15_
  14.9 1.6 %collective-permute-start.5 = (bf16[8,64,128]{2,1,0:T(8,128)(2,1)S(1)}, bf16[8,64,128]{2,1,0:T(8,128)(2,1)S(1)}, u32[]{:S(2)}, u32[]{:S(2)}) collective-permute-start(bf16[8,64,128]{2,1,0:T(8,128)(2,1)S(1)} %collective-permute-done.1.refs_15_), channel_id=1, source_target_pairs={{0,4},{1,3},{2,0},{3,7},{4,8},{5,1},{6,2},{7,11},{8,12},{9,5},{10,... | collective-permute-start | bytes 393224 | tf_op jit(solution)/shard_map/ppermute | solution.py:105
  16.5 0.0 copy-start.18
  16.5 3.5 %left.1.x_ref = bf16[112,64,64]{2,1,0:T(8,128)(2,1)} custom-call(bf16[16,7,64,64]{3,2,1,0:T(8,128)(2,1)} %a_ref.1, bf16[16,64,64]{2,1,0:T(8,128)(2,1)} %p_ref.3), custom_call_target="tpu_custom_call" | custom-call | tf_op jit(solution)/shard_map/left/pallas_call | solution.py:119
  20.0 0.0 copy-done.1
  20.0 0.0 copy-done.2
  20.0 0.0 collective-permute-start.4
  20.0 0.5 %collective-permute-start.8 = (bf16[8,64,128]{2,1,0:T(8,128)(2,1)S(1)}, bf16[8,64,128]{2,1,0:T(8,128)(2,1)S(1)}, u32[]{:S(2)}, u32[]{:S(2)}) collective-permute-start(bf16[8,64,128]{2,1,0:T(8,128)(2,1)S(1)} %collective-permute-done.7.refs_12_), channel_id=1, source_target_pairs={{0,1},{1,0},{2,3},{3,2},{4,5},{5,4},{6,7},{7,6},{8,9},{9,8},{10,11... | collective-permute-start | bytes 393224 | tf_op jit(solution)/shard_map/ppermute | solution.py:107
  20.5 0.0 collective-permute-done.11.refs_10_
  20.5 1.6 %collective-permute-start.13 = (bf16[8,64,128]{2,1,0:T(8,128)(2,1)S(1)}, bf16[8,64,128]{2,1,0:T(8,128)(2,1)S(1)}, u32[]{:S(2)}, u32[]{:S(2)}) collective-permute-start(bf16[8,64,128]{2,1,0:T(8,128)(2,1)S(1)} %collective-permute-done.11.refs_10_), channel_id=1, source_target_pairs={{0,4},{1,3},{2,0},{3,7},{4,8},{5,1},{6,2},{7,11},{8,12},{9,5},{10,... | collective-permute-start | bytes 393224 | tf_op jit(solution)/shard_map/ppermute | solution.py:103
  22.1 0.0 collective-permute-done.5.refs_13_
  22.1 1.5 %collective-permute-start.9 = (bf16[8,64,128]{2,1,0:T(8,128)(2,1)S(1)}, bf16[8,64,128]{2,1,0:T(8,128)(2,1)S(1)}, u32[]{:S(2)}, u32[]{:S(2)}) collective-permute-start(bf16[8,64,128]{2,1,0:T(8,128)(2,1)S(1)} %collective-permute-done.5.refs_13_), channel_id=1, source_target_pairs={{0,4},{1,3},{2,0},{3,7},{4,8},{5,1},{6,2},{7,11},{8,12},{9,5},{10,... | collective-permute-start | bytes 393224 | tf_op jit(solution)/shard_map/ppermute | solution.py:105
  23.6 0.0 copy-done.19
  23.7 0.1 collective-permute-start.2
  23.7 0.0 collective-permute-done.4.refs_3_
  23.7 0.0 copy-start.7
  23.8 0.5 %collective-permute-start.12 = (bf16[8,64,128]{2,1,0:T(8,128)(2,1)S(1)}, bf16[8,64,128]{2,1,0:T(8,128)(2,1)S(1)}, u32[]{:S(2)}, u32[]{:S(2)}) collective-permute-start(bf16[8,64,128]{2,1,0:T(8,128)(2,1)S(1)} %collective-permute-done.11.refs_10_), channel_id=1, source_target_pairs={{0,1},{1,0},{2,3},{3,2},{4,5},{5,4},{6,7},{7,6},{8,9},{9,8},{10,11... | collective-permute-start | bytes 393224 | tf_op jit(solution)/shard_map/ppermute | solution.py:107
  24.2 0.0 collective-permute-done.8.refs_5_
  24.2 0.1 collective-permute-start.6
  24.3 1.2 %collective-permute-done.13.refs_8_ = bf16[8,64,128]{2,1,0:T(8,128)(2,1)S(1)} collective-permute-done((bf16[8,64,128]{2,1,0:T(8,128)(2,1)S(1)}, bf16[8,64,128]{2,1,0:T(8,128)(2,1)S(1)}, u32[]{:S(2)}, u32[]{:S(2)}) %collective-permute-start.13) | collective-permute-done | bytes 131104 | tf_op jit(solution)/shard_map/ppermute | solution.py:103
  25.5 0.0 collective-permute-start.14
  25.5 1.6 %collective-permute-done.9.refs_11_ = bf16[8,64,128]{2,1,0:T(8,128)(2,1)S(1)} collective-permute-done((bf16[8,64,128]{2,1,0:T(8,128)(2,1)S(1)}, bf16[8,64,128]{2,1,0:T(8,128)(2,1)S(1)}, u32[]{:S(2)}, u32[]{:S(2)}) %collective-permute-start.9) | collective-permute-done | bytes 131104 | tf_op jit(solution)/shard_map/ppermute | solution.py:105
  27.1 0.0 collective-permute-start.10
  27.1 0.6 %fusion.14.code_ref = s32[7,16]{1,0:T(8,128)} fusion(s32[16,7]{0,1:T(8,128)S(1)} %copy-done.16, s32[16,7]{0,1:T(8,128)S(1)} %copy-done.17, s32[16,7]{0,1:T(8,128)S(1)} %copy-done.18, s32[16]{0:T(128)S(1)} %fusion.25, s32[]{:T(128)S(6)} %select_n.60, s32[]{:T(128)S(6)} %sub.58, s32[]{:T(128)S(6)} %add.74), kind=kLoop, calls=%fused_computation.33 | loop fusion | flops 9632 | bytes 1868 | tf_op jit(solution)/shard_map/add | solution.py:133
  27.7 0.0 collective-permute-done.2.refs_2_
  27.8 0.0 collective-permute-done.12.refs_7_
  27.8 0.0 collective-permute-done.6.refs_4_
  27.8 0.0 collective-permute-done.14.refs_9_
  27.8 0.0 copy-start.14
  27.8 0.6 %collective-permute-done.10.refs_6_ = bf16[8,64,128]{2,1,0:T(8,128)(2,1)S(1)} collective-permute-done((bf16[8,64,128]{2,1,0:T(8,128)(2,1)S(1)}, bf16[8,64,128]{2,1,0:T(8,128)(2,1)S(1)}, u32[]{:S(2)}, u32[]{:S(2)}) %collective-permute-start.10) | collective-permute-done | bytes 131104 | tf_op jit(solution)/shard_map/ppermute | solution.py:107
  28.4 0.0 copy-done.5
  28.4 0.0 copy-done.7
  28.5 0.1 copy-done.14
  28.6 0.6 %copy-done.15 = bf16[8,64,128]{2,1,0:T(8,128)(2,1)} copy-done((bf16[8,64,128]{2,1,0:T(8,128)(2,1)}, bf16[8,64,128]{2,1,0:T(8,128)(2,1)S(1)}, u32[]{:S(2)}) %copy-start.15) | copy-done | bytes 131096
  29.2 4.4 %sum.1 = (f32[14,64,128]{2,1,0:T(8,128)}, bf16[1,14,64,128]{3,2,1,0:T(8,128)(2,1)}) custom-call(s32[7,16]{1,0:T(8,128)} %fusion.14.code_ref, bf16[112,64,64]{2,1,0:T(8,128)(2,1)} %left.1.x_ref, bf16[8,64,128]{2,1,0:T(8,128)(2,1)} %pack.1.refs_0_, bf16[8,64,128]{2,1,0:T(8,128)(2,1)} %copy-done.2, bf16[8,64,128]{2,1,0:T(8,128)(2,1)} %copy-done.11, ...), custom_call_target="tpu_custom_call" | custom-call | tf_op jit(solution)/shard_map/sum/pallas_call | solution.py:137
  33.6 1.5 %collective-permute-start.15 = (bf16[14,64,128]{2,1,0:T(8,128)(2,1)}, bf16[14,64,128]{2,1,0:T(8,128)(2,1)S(1)}, u32[]{:S(2)}, u32[]{:S(2)}) collective-permute-start(bf16[14,64,128]{2,1,0:T(8,128)(2,1)} %bitcast.48), channel_id=1, source_target_pairs={{0,16},{16,0},{1,17},{17,1},{2,18},{18,2},{3,19},{19,3},{4,20},{20... | collective-permute-start | bytes 688136 | tf_op jit(solution)/shard_map/ppermute | solution.py:152
  35.1 6.7 %collective-permute-done.15.refs_0_ = bf16[14,64,128]{2,1,0:T(8,128)(2,1)S(1)} collective-permute-done((bf16[14,64,128]{2,1,0:T(8,128)(2,1)}, bf16[14,64,128]{2,1,0:T(8,128)(2,1)S(1)}, u32[]{:S(2)}, u32[]{:S(2)}) %collective-permute-start.15) | collective-permute-done | bytes 229408 | tf_op jit(solution)/shard_map/ppermute | solution.py:152
  41.8 0.7 %copy-done = bf16[14,64,128]{2,1,0:T(8,128)(2,1)} copy-done((bf16[14,64,128]{2,1,0:T(8,128)(2,1)}, bf16[14,64,128]{2,1,0:T(8,128)(2,1)S(1)}, u32[]{:S(2)}) %copy-start) | copy-done | bytes 229400
  42.5 2.0 %add.165 = bf16[28,64,64]{2,1,0:T(8,128)(2,1)} custom-call(f32[14,64,128]{2,1,0:T(8,128)} %get-tuple-element.7.own_ref, bf16[14,64,128]{2,1,0:T(8,128)(2,1)} %copy-done), custom_call_target="tpu_custom_call" | custom-call | tf_op jit(solution)/shard_map/add/pallas_call | solution.py:155
  (32 shorter events, 0.1 us)
Async XLA Ops:
  1.7 6.2 %collective-permute-start.3 = (bf16[8,64,128]{2,1,0:T(8,128)(2,1)}, bf16[8,64,128]{2,1,0:T(8,128)(2,1)S(1)}, u32[]{:S(2)}, u32[]{:S(2)}) collective-permute-start(bf16[8,64,128]{2,1,0:T(8,128)(2,1)} %pack.1.refs_0_), channel_id=1, source_target_pairs={{0,4},{1,3},{2,0},{3,7},{4,8},{5,1},{6,2},{7,11},{8,12},{9,5},{10,... | collective-permute-start | bytes 393224 | tf_op jit(solution)/shard_map/ppermute | solution.py:103
  4.8 5.2 %collective-permute-start = (bf16[8,64,128]{2,1,0:T(8,128)(2,1)}, bf16[8,64,128]{2,1,0:T(8,128)(2,1)S(1)}, u32[]{:S(2)}, u32[]{:S(2)}) collective-permute-start(bf16[8,64,128]{2,1,0:T(8,128)(2,1)} %pack.1.refs_0_), channel_id=1, source_target_pairs={{0,1},{1,0},{2,3},{3,2},{4,5},{5,4},{6,7},{7,6},{8,9},{9,8},{10,11... | collective-permute-start | bytes 393224 | tf_op jit(solution)/shard_map/ppermute | solution.py:100
  7.9 12.2 %copy-start.1 = (bf16[8,64,128]{2,1,0:T(8,128)(2,1)}, bf16[8,64,128]{2,1,0:T(8,128)(2,1)S(1)}, u32[]{:S(2)}) copy-start(bf16[8,64,128]{2,1,0:T(8,128)(2,1)S(1)} %collective-permute-done.3.refs_14_) | copy-start | bytes 393220
  7.9 5.0 %collective-permute-start.7 = (bf16[8,64,128]{2,1,0:T(8,128)(2,1)S(1)}, bf16[8,64,128]{2,1,0:T(8,128)(2,1)S(1)}, u32[]{:S(2)}, u32[]{:S(2)}) collective-permute-start(bf16[8,64,128]{2,1,0:T(8,128)(2,1)S(1)} %collective-permute-done.3.refs_14_), channel_id=1, source_target_pairs={{0,4},{1,3},{2,0},{3,7},{4,8},{5,1},{6,2},{7,11},{8,12},{9,5},{10,... | collective-permute-start | bytes 393224 | tf_op jit(solution)/shard_map/ppermute | solution.py:103
  9.9 10.1 %copy-start.2 = (bf16[8,64,128]{2,1,0:T(8,128)(2,1)}, bf16[8,64,128]{2,1,0:T(8,128)(2,1)S(1)}, u32[]{:S(2)}) copy-start(bf16[8,64,128]{2,1,0:T(8,128)(2,1)S(1)} %collective-permute-done.refs_1_) | copy-start | bytes 393220
  9.9 5.0 %collective-permute-start.1 = (bf16[8,64,128]{2,1,0:T(8,128)(2,1)S(1)}, bf16[8,64,128]{2,1,0:T(8,128)(2,1)S(1)}, u32[]{:S(2)}, u32[]{:S(2)}) collective-permute-start(bf16[8,64,128]{2,1,0:T(8,128)(2,1)S(1)} %collective-permute-done.refs_1_), channel_id=1, source_target_pairs={{0,4},{1,3},{2,0},{3,7},{4,8},{5,1},{6,2},{7,11},{8,12},{9,5},{10,... | collective-permute-start | bytes 393224 | tf_op jit(solution)/shard_map/ppermute | solution.py:105
  12.8 7.2 %copy-start.3 = (bf16[8,64,128]{2,1,0:T(8,128)(2,1)}, bf16[8,64,128]{2,1,0:T(8,128)(2,1)S(1)}, u32[]{:S(2)}) copy-start(bf16[8,64,128]{2,1,0:T(8,128)(2,1)S(1)} %collective-permute-done.7.refs_12_) | copy-start | bytes 393220
  12.8 7.7 %collective-permute-start.11 = (bf16[8,64,128]{2,1,0:T(8,128)(2,1)S(1)}, bf16[8,64,128]{2,1,0:T(8,128)(2,1)S(1)}, u32[]{:S(2)}, u32[]{:S(2)}) collective-permute-start(bf16[8,64,128]{2,1,0:T(8,128)(2,1)S(1)} %collective-permute-done.7.refs_12_), channel_id=1, source_target_pairs={{0,4},{1,3},{2,0},{3,7},{4,8},{5,1},{6,2},{7,11},{8,12},{9,5},{10,... | collective-permute-start | bytes 393224 | tf_op jit(solution)/shard_map/ppermute | solution.py:103
  14.9 8.7 %copy-start.4 = (bf16[8,64,128]{2,1,0:T(8,128)(2,1)}, bf16[8,64,128]{2,1,0:T(8,128)(2,1)S(1)}, u32[]{:S(2)}) copy-start(bf16[8,64,128]{2,1,0:T(8,128)(2,1)S(1)} %collective-permute-done.1.refs_15_) | copy-start | bytes 393220
  14.9 7.2 %collective-permute-start.5 = (bf16[8,64,128]{2,1,0:T(8,128)(2,1)S(1)}, bf16[8,64,128]{2,1,0:T(8,128)(2,1)S(1)}, u32[]{:S(2)}, u32[]{:S(2)}) collective-permute-start(bf16[8,64,128]{2,1,0:T(8,128)(2,1)S(1)} %collective-permute-done.1.refs_15_), channel_id=1, source_target_pairs={{0,4},{1,3},{2,0},{3,7},{4,8},{5,1},{6,2},{7,11},{8,12},{9,5},{10,... | collective-permute-start | bytes 393224 | tf_op jit(solution)/shard_map/ppermute | solution.py:105
  16.5 7.1 %copy-start.19 = (s32[16]{0:T(128)S(1)}, s32[16]{0:T(128)}, u32[]{:S(2)}) copy-start(s32[16]{0:T(128)} %param.12) | copy-start | bytes 196
  16.5 7.1 %copy-start.20 = (s32[16,1]{0,1:T(1,128)S(1)}, s32[16,1]{0,1:T(1,128)}, u32[]{:S(2)}) copy-start(s32[16,1]{0,1:T(1,128)} %param.11) | copy-start | bytes 196
  16.5 10.6 %copy-start.16 = (s32[16,7]{0,1:T(8,128)S(1)}, s32[16,7]{0,1:T(8,128)}, u32[]{:S(2)}) copy-start(s32[16,7]{0,1:T(8,128)} %param.13) | copy-start | bytes 1348
  16.5 10.6 %copy-start.17 = (s32[16,7]{0,1:T(8,128)S(1)}, s32[16,7]{0,1:T(8,128)}, u32[]{:S(2)}) copy-start(s32[16,7]{0,1:T(8,128)} %param.10) | copy-start | bytes 1348
  16.5 10.6 %copy-start.18 = (s32[16,7]{0,1:T(8,128)S(1)}, s32[16,7]{0,1:T(8,128)}, u32[]{:S(2)}) copy-start(s32[16,7]{0,1:T(8,128)} %param.9) | copy-start | bytes 1348
  20.0 3.7 %collective-permute-start.4 = (bf16[8,64,128]{2,1,0:T(8,128)(2,1)S(1)}, bf16[8,64,128]{2,1,0:T(8,128)(2,1)S(1)}, u32[]{:S(2)}, u32[]{:S(2)}) collective-permute-start(bf16[8,64,128]{2,1,0:T(8,128)(2,1)S(1)} %collective-permute-done.3.refs_14_), channel_id=1, source_target_pairs={{0,1},{1,0},{2,3},{3,2},{4,5},{5,4},{6,7},{7,6},{8,9},{9,8},{10,11... | collective-permute-start | bytes 393224 | tf_op jit(solution)/shard_map/ppermute | solution.py:107
  20.0 4.2 %collective-permute-start.8 = (bf16[8,64,128]{2,1,0:T(8,128)(2,1)S(1)}, bf16[8,64,128]{2,1,0:T(8,128)(2,1)S(1)}, u32[]{:S(2)}, u32[]{:S(2)}) collective-permute-start(bf16[8,64,128]{2,1,0:T(8,128)(2,1)S(1)} %collective-permute-done.7.refs_12_), channel_id=1, source_target_pairs={{0,1},{1,0},{2,3},{3,2},{4,5},{5,4},{6,7},{7,6},{8,9},{9,8},{10,11... | collective-permute-start | bytes 393224 | tf_op jit(solution)/shard_map/ppermute | solution.py:107
  20.5 7.9 %copy-start.5 = (bf16[8,64,128]{2,1,0:T(8,128)(2,1)}, bf16[8,64,128]{2,1,0:T(8,128)(2,1)S(1)}, u32[]{:S(2)}) copy-start(bf16[8,64,128]{2,1,0:T(8,128)(2,1)S(1)} %collective-permute-done.11.refs_10_) | copy-start | bytes 393220
  20.5 5.0 %collective-permute-start.13 = (bf16[8,64,128]{2,1,0:T(8,128)(2,1)S(1)}, bf16[8,64,128]{2,1,0:T(8,128)(2,1)S(1)}, u32[]{:S(2)}, u32[]{:S(2)}) collective-permute-start(bf16[8,64,128]{2,1,0:T(8,128)(2,1)S(1)} %collective-permute-done.11.refs_10_), channel_id=1, source_target_pairs={{0,4},{1,3},{2,0},{3,7},{4,8},{5,1},{6,2},{7,11},{8,12},{9,5},{10,... | collective-permute-start | bytes 393224 | tf_op jit(solution)/shard_map/ppermute | solution.py:103
  22.1 6.3 %copy-start.6 = (bf16[8,64,128]{2,1,0:T(8,128)(2,1)}, bf16[8,64,128]{2,1,0:T(8,128)(2,1)S(1)}, u32[]{:S(2)}) copy-start(bf16[8,64,128]{2,1,0:T(8,128)(2,1)S(1)} %collective-permute-done.5.refs_13_) | copy-start | bytes 393220
  22.1 5.0 %collective-permute-start.9 = (bf16[8,64,128]{2,1,0:T(8,128)(2,1)S(1)}, bf16[8,64,128]{2,1,0:T(8,128)(2,1)S(1)}, u32[]{:S(2)}, u32[]{:S(2)}) collective-permute-start(bf16[8,64,128]{2,1,0:T(8,128)(2,1)S(1)} %collective-permute-done.5.refs_13_), channel_id=1, source_target_pairs={{0,4},{1,3},{2,0},{3,7},{4,8},{5,1},{6,2},{7,11},{8,12},{9,5},{10,... | collective-permute-start | bytes 393224 | tf_op jit(solution)/shard_map/ppermute | solution.py:105
  23.7 4.1 %collective-permute-start.2 = (bf16[8,64,128]{2,1,0:T(8,128)(2,1)S(1)}, bf16[8,64,128]{2,1,0:T(8,128)(2,1)S(1)}, u32[]{:S(2)}, u32[]{:S(2)}) collective-permute-start(bf16[8,64,128]{2,1,0:T(8,128)(2,1)S(1)} %collective-permute-done.1.refs_15_), channel_id=1, source_target_pairs={{0,1},{1,0},{2,3},{3,2},{4,5},{5,4},{6,7},{7,6},{8,9},{9,8},{10,11... | collective-permute-start | bytes 393224 | tf_op jit(solution)/shard_map/ppermute | solution.py:107
  23.7 4.7 %copy-start.7 = (bf16[8,64,128]{2,1,0:T(8,128)(2,1)}, bf16[8,64,128]{2,1,0:T(8,128)(2,1)S(1)}, u32[]{:S(2)}) copy-start(bf16[8,64,128]{2,1,0:T(8,128)(2,1)S(1)} %collective-permute-done.4.refs_3_) | copy-start | bytes 393220
  23.8 4.0 %collective-permute-start.12 = (bf16[8,64,128]{2,1,0:T(8,128)(2,1)S(1)}, bf16[8,64,128]{2,1,0:T(8,128)(2,1)S(1)}, u32[]{:S(2)}, u32[]{:S(2)}) collective-permute-start(bf16[8,64,128]{2,1,0:T(8,128)(2,1)S(1)} %collective-permute-done.11.refs_10_), channel_id=1, source_target_pairs={{0,1},{1,0},{2,3},{3,2},{4,5},{5,4},{6,7},{7,6},{8,9},{9,8},{10,11... | collective-permute-start | bytes 393224 | tf_op jit(solution)/shard_map/ppermute | solution.py:107
  24.2 4.2 %copy-start.8 = (bf16[8,64,128]{2,1,0:T(8,128)(2,1)}, bf16[8,64,128]{2,1,0:T(8,128)(2,1)S(1)}, u32[]{:S(2)}) copy-start(bf16[8,64,128]{2,1,0:T(8,128)(2,1)S(1)} %collective-permute-done.8.refs_5_) | copy-start | bytes 393220
  24.2 3.5 %collective-permute-start.6 = (bf16[8,64,128]{2,1,0:T(8,128)(2,1)S(1)}, bf16[8,64,128]{2,1,0:T(8,128)(2,1)S(1)}, u32[]{:S(2)}, u32[]{:S(2)}) collective-permute-start(bf16[8,64,128]{2,1,0:T(8,128)(2,1)S(1)} %collective-permute-done.5.refs_13_), channel_id=1, source_target_pairs={{0,1},{1,0},{2,3},{3,2},{4,5},{5,4},{6,7},{7,6},{8,9},{9,8},{10,11... | collective-permute-start | bytes 393224 | tf_op jit(solution)/shard_map/ppermute | solution.py:107
  25.5 3.0 %copy-start.9 = (bf16[8,64,128]{2,1,0:T(8,128)(2,1)}, bf16[8,64,128]{2,1,0:T(8,128)(2,1)S(1)}, u32[]{:S(2)}) copy-start(bf16[8,64,128]{2,1,0:T(8,128)(2,1)S(1)} %collective-permute-done.13.refs_8_) | copy-start | bytes 393220
  25.5 2.3 %collective-permute-start.14 = (bf16[8,64,128]{2,1,0:T(8,128)(2,1)S(1)}, bf16[8,64,128]{2,1,0:T(8,128)(2,1)S(1)}, u32[]{:S(2)}, u32[]{:S(2)}) collective-permute-start(bf16[8,64,128]{2,1,0:T(8,128)(2,1)S(1)} %collective-permute-done.13.refs_8_), channel_id=1, source_target_pairs={{0,1},{1,0},{2,3},{3,2},{4,5},{5,4},{6,7},{7,6},{8,9},{9,8},{10,11... | collective-permute-start | bytes 393224 | tf_op jit(solution)/shard_map/ppermute | solution.py:109
  27.1 1.4 %copy-start.10 = (bf16[8,64,128]{2,1,0:T(8,128)(2,1)}, bf16[8,64,128]{2,1,0:T(8,128)(2,1)S(1)}, u32[]{:S(2)}) copy-start(bf16[8,64,128]{2,1,0:T(8,128)(2,1)S(1)} %collective-permute-done.9.refs_11_) | copy-start | bytes 393220
  27.1 1.3 %collective-permute-start.10 = (bf16[8,64,128]{2,1,0:T(8,128)(2,1)S(1)}, bf16[8,64,128]{2,1,0:T(8,128)(2,1)S(1)}, u32[]{:S(2)}, u32[]{:S(2)}) collective-permute-start(bf16[8,64,128]{2,1,0:T(8,128)(2,1)S(1)} %collective-permute-done.9.refs_11_), channel_id=1, source_target_pairs={{0,1},{1,0},{2,3},{3,2},{4,5},{5,4},{6,7},{7,6},{8,9},{9,8},{10,11... | collective-permute-start | bytes 393224 | tf_op jit(solution)/shard_map/ppermute | solution.py:107
  27.7 0.7 %copy-start.11 = (bf16[8,64,128]{2,1,0:T(8,128)(2,1)}, bf16[8,64,128]{2,1,0:T(8,128)(2,1)S(1)}, u32[]{:S(2)}) copy-start(bf16[8,64,128]{2,1,0:T(8,128)(2,1)S(1)} %collective-permute-done.2.refs_2_) | copy-start | bytes 393220
  27.8 0.7 %copy-start.12 = (bf16[8,64,128]{2,1,0:T(8,128)(2,1)}, bf16[8,64,128]{2,1,0:T(8,128)(2,1)S(1)}, u32[]{:S(2)}) copy-start(bf16[8,64,128]{2,1,0:T(8,128)(2,1)S(1)} %collective-permute-done.12.refs_7_) | copy-start | bytes 393220
  27.8 0.7 %copy-start.13 = (bf16[8,64,128]{2,1,0:T(8,128)(2,1)}, bf16[8,64,128]{2,1,0:T(8,128)(2,1)S(1)}, u32[]{:S(2)}) copy-start(bf16[8,64,128]{2,1,0:T(8,128)(2,1)S(1)} %collective-permute-done.6.refs_4_) | copy-start | bytes 393220
  27.8 0.8 %copy-start.14 = (bf16[8,64,128]{2,1,0:T(8,128)(2,1)}, bf16[8,64,128]{2,1,0:T(8,128)(2,1)S(1)}, u32[]{:S(2)}) copy-start(bf16[8,64,128]{2,1,0:T(8,128)(2,1)S(1)} %collective-permute-done.14.refs_9_) | copy-start | bytes 393220
  28.6 0.6 %copy-start.15 = (bf16[8,64,128]{2,1,0:T(8,128)(2,1)}, bf16[8,64,128]{2,1,0:T(8,128)(2,1)S(1)}, u32[]{:S(2)}) copy-start(bf16[8,64,128]{2,1,0:T(8,128)(2,1)S(1)} %collective-permute-done.10.refs_6_) | copy-start | bytes 393220
  33.6 8.2 %collective-permute-start.15 = (bf16[14,64,128]{2,1,0:T(8,128)(2,1)}, bf16[14,64,128]{2,1,0:T(8,128)(2,1)S(1)}, u32[]{:S(2)}, u32[]{:S(2)}) collective-permute-start(bf16[14,64,128]{2,1,0:T(8,128)(2,1)} %bitcast.48), channel_id=1, source_target_pairs={{0,16},{16,0},{1,17},{17,1},{2,18},{18,2},{3,19},{19,3},{4,20},{20... | collective-permute-start | bytes 688136 | tf_op jit(solution)/shard_map/ppermute | solution.py:152
  41.8 0.7 %copy-start = (bf16[14,64,128]{2,1,0:T(8,128)(2,1)}, bf16[14,64,128]{2,1,0:T(8,128)(2,1)S(1)}, u32[]{:S(2)}) copy-start(bf16[14,64,128]{2,1,0:T(8,128)(2,1)S(1)} %collective-permute-done.15.refs_0_) | copy-start | bytes 688132

commit v2 on v1

v2 whole, which is shorter than its diff:
```python
import jax
import jax.numpy as jnp
from jax import lax
from jax.experimental import pallas as pl
from jax.experimental.pallas import tpu as pltpu
from jax.sharding import PartitionSpec as P

KC = 7
NC_DEV = 4
VMEM = pl.BlockSpec(memory_space=pltpu.VMEM)
SMEM = pl.BlockSpec(memory_space=pltpu.SMEM)
HBM = pl.BlockSpec(memory_space=pltpu.HBM)
LIMIT = 1 << 20
PARTS = 8


def keep(*arrays):
    return [pltpu.with_memory_space_constraint(array, pltpu.VMEM) for array in arrays]


def routes(columns):
    near = {4: 0, 12: 0, 2: 0, 6: 4, 10: 2, 8: 12, 14: 12}
    order = [key for key in near if key < columns]
    far = list(range(16, columns, 2))
    parents = {key: near[key] for key in order} | {key: key & 15 for key in far}
    groups = [[0, 2, 4, 12], [10, 6], [8, 14], far]
    groups = [[key for key in group if key < columns] for group in groups]
    return order + far, parents, [group for group in groups if group]


def slots(columns):
    keys = [key ^ core for group in routes(columns)[2] for core in range(2) for key in group]
    return {key: slot for slot, key in enumerate(keys)}


def pack_kernel(p_ref, out_ref, kept_ref):
    pairs, _, _ = out_ref.shape
    kept_ref[...] = p_ref[...]
    for j in range(pairs):
        out_ref[j] = jnp.concatenate([p_ref[j], p_ref[j + pairs]], axis=1)


def merge_kernel(*refs):
    *pieces, out_ref = refs
    start = 0
    for piece in pieces:
        out_ref[start : start + piece.shape[0]] = piece[...]
        start += piece.shape[0]


def codes(peer_ref, place_ref, owner_ref, slot_ref, row_ref):
    rows = peer_ref.shape[1]
    columns, regions = lax.axis_size("col"), lax.axis_size("row")
    pairs, lanes = rows // 2, NC_DEV * KC
    me, region = lax.axis_index("col"), lax.axis_index("row")
    key, place = peer_ref[...] ^ me, place_ref[...]
    piece = jnp.zeros_like(key)
    for value, slot in slots(columns).items():
        piece = jnp.where(key == value, slot, piece)
    high = jnp.where(place < pairs, 0, 1)
    source = piece * pairs + place - high * pairs
    relative = owner_ref[...] - region
    relative = jnp.where(relative < 0, relative + regions, relative)
    target = (relative * NC_DEV + row_ref[...]) * KC + slot_ref[...]
    return source * 65536 + target + high * (regions * lanes)


def left_kernel(p_ref, a_ref, peer_ref, place_ref, owner_ref, slot_ref, row_ref, x_ref, out_ref, *held):
    *index_held, a_held, code_ref, index_sems, sems, code_sem = held
    rows, entries = a_ref.shape[:2]
    parts = sems.shape[0]
    step = rows // parts
    index_copies = [
        pltpu.make_async_copy(source, target, index_sems.at[n])
        for n, (source, target) in enumerate(
            zip((peer_ref, place_ref, owner_ref, slot_ref, row_ref), index_held)
        )
    ]
    for copy in index_copies:
        copy.start()
    copies = []
    for n in range(parts):
        part = pl.ds(n * step, step)
        copies.append(pltpu.make_async_copy(a_ref.at[part], a_held.at[part], sems.at[n]))
        copies[n].start()
    for copy in index_copies:
        copy.wait()
    code_ref[...] = codes(*index_held)
    code_copy = pltpu.make_async_copy(code_ref, out_ref, code_sem)
    code_copy.start()
    for n in range(parts):
        copies[n].wait()
        for i in range(n * step, (n + 1) * step):
            for k in range(entries):
                x = lax.dot_general(
                    p_ref[i], a_held[i, k], (((0,), (0,)), ((), ())),
                    preferred_element_type=jnp.float32,
                )
                x_ref[i * entries + k] = x.astype(x_ref.dtype)
    code_copy.wait()


def fold(acc_ref, base, half, j, low):
    rows = acc_ref.shape[0] // 2
    first = jnp.where(low, acc_ref[base + j], acc_ref[rows + base + half + j])
    second = jnp.where(low, acc_ref[base + half + j], acc_ref[rows + base + j])
    order = first.shape[1] // 2
    return first + pltpu.roll(second, order, axis=1)


def sum_kernel(code_ref, x_ref, *refs):
    *pieces, own_ref, sent_ref, gathered_ref, acc_ref = refs
    entries, rows = code_ref.shape
    order, width = pieces[0].shape[1:]
    acc_ref[...] = jnp.zeros_like(acc_ref)
    merge_kernel(*pieces, gathered_ref)
    for i in range(rows):
        for k in range(entries):
            code = code_ref[k, i]
            source, target = code >> 16, code & 0xFFFF
            acc_ref[target] += jnp.dot(
                x_ref[i * entries + k], gathered_ref[source], preferred_element_type=jnp.float32
            )
    lanes = lax.broadcasted_iota(jnp.int32, (order, width), 1)
    low = lanes < width // 2
    half = own_ref.shape[0]
    for j in range(half):
        own_ref[j] = fold(acc_ref, 0, half, j, low)
    for n in range(sent_ref.shape[0]):
        for j in range(half):
            sent_ref[n, j] = fold(acc_ref, 2 * half * (n + 1), half, j, low).astype(sent_ref.dtype)


def add_kernel(own_ref, *refs):
    *received, out_ref = refs
    half, _, width = own_ref.shape
    for j in range(half):
        total = own_ref[j]
        for ref in received:
            total = total + ref[j].astype(jnp.float32)
        out_ref[j] = total[:, : width // 2].astype(out_ref.dtype)
        out_ref[half + j] = pltpu.roll(total, width // 2, axis=1)[:, : width // 2].astype(out_ref.dtype)


def call(kernel, out_shape, in_specs, out_specs, scratch_shapes=(), limit=LIMIT):
    return pl.pallas_call(
        kernel, out_shape=out_shape, in_specs=in_specs, out_specs=out_specs,
        scratch_shapes=scratch_shapes,
        compiler_params=pltpu.CompilerParams(vmem_limit_bytes=limit),
    )


def local(a_blocks, p_blocks, a_peer, a_local, agg_owner, agg_local, entry_slot):
    rows, entries, order, _ = a_blocks.shape
    columns, regions = lax.axis_size("col"), lax.axis_size("row")
    pairs = rows // 2
    lanes = NC_DEV * KC

    def exchange(array, bits):
        return lax.ppermute(array, "col", [(i, i ^ bits) for i in range(columns)])

    own, kept = call(
        pack_kernel,
        (
            pltpu.VMEM((pairs, order, 2 * order), p_blocks.dtype),
            pltpu.VMEM(p_blocks.shape, p_blocks.dtype),
        ),
        [VMEM], (VMEM, VMEM),
    )(*keep(p_blocks))

    order_of, parents, groups = routes(columns)
    held = {0: own}
    for key in order_of:
        held[key] = exchange(held[parents[key]], key ^ parents[key])
    pieces = []
    for group in groups:
        mine = call(
            merge_kernel, pltpu.VMEM((len(group) * pairs, order, 2 * order), own.dtype),
            [VMEM] * len(group), VMEM,
        )(*keep(*[held[key] for key in group]))
        pieces += [mine, exchange(mine, 1)]

    indices = (a_peer.T, a_local.T, agg_owner.T, entry_slot.T, agg_local[None])
    x, code = call(
        left_kernel,
        (
            pltpu.VMEM((rows * entries, order, order), jnp.bfloat16),
            pltpu.SMEM((entries, rows), jnp.int32),
        ),
        [VMEM] + [HBM] * 6, (VMEM, SMEM),
        [pltpu.VMEM(array.shape, array.dtype) for array in indices]
        + [
            pltpu.VMEM(a_blocks.shape, a_blocks.dtype), pltpu.VMEM((entries, rows), jnp.int32),
            pltpu.SemaphoreType.DMA((len(indices),)), pltpu.SemaphoreType.DMA((PARTS,)),
            pltpu.SemaphoreType.DMA(()),
        ],
        limit=a_blocks.size * 4 + LIMIT,
    )(*keep(kept), *[pltpu.with_memory_space_constraint(v, pltpu.HBM) for v in (a_blocks, *indices)])

    half = lanes // 2
    width = 2 * order
    scratch = (columns * pairs * 2 + 2 * regions * lanes * 4) * order * width
    own_sum, sent = call(
        sum_kernel,
        (
            pltpu.VMEM((half, order, width), jnp.float32),
            pltpu.VMEM((regions - 1, half, order, width), jnp.bfloat16),
        ),
        [SMEM] + [VMEM] * (1 + len(pieces)), (VMEM, VMEM),
        [
            pltpu.VMEM((columns * pairs, order, width), p_blocks.dtype),
            pltpu.VMEM((2 * regions * lanes, order, width), jnp.float32),
        ],
        limit=scratch + LIMIT,
    )(pltpu.with_memory_space_constraint(code, pltpu.SMEM), *keep(x, *pieces))

    received = [
        lax.ppermute(sent[n - 1], "row", [(i, (i + n) % regions) for i in range(regions)])
        for n in range(1, regions)
    ]
    out = call(
        add_kernel, jax.ShapeDtypeStruct((lanes, order, order), jnp.bfloat16),
        [VMEM] * regions, VMEM, limit=4 << 20,
    )(*keep(own_sum, *received))
    return out.reshape(NC_DEV, KC, order, order)


def solution(mesh):
    in_specs = (
        P(("row", "col"), None, None, None),
        P(("row", "col"), None, None),
        P(("row", "col"), None),
        P(("row", "col"), None),
        P(("row", "col"), None),
        P(("row", "col")),
        P(("row", "col"), None),
    )
    out_specs = P(("row", "col"), None, None, None)

    return jax.shard_map(local, mesh=mesh, in_specs=in_specs, out_specs=out_specs, check_vma=False)
```

time: 44.7 us -> 38 us (0.85)
  Pallas kernels: 11.6 us -> 6.05 us
  waiting for transfers between devices: 14.5 us -> 17.4 us
  starting transfers between devices: 16.1 us -> 13.3 us
  other arithmetic: 0.64 us -> 0 us
  local copies, waits for them, and re-layouts: 1.45 us -> 0.95 us
    pallas_call x4 -> x7, Pallas kernels: 11.6 us -> 6.05 us  [the longest x1 3.48 us: local(): call(left_kernel, (pltpu.VMEM((rows * entries, order, order), jnp.bfloat1...]
    ppermute x15 -> x10, waiting for transfers between devices: 7.79 us -> 11.4 us  [exchange(): return lax.ppermute(array, 'col', [(i, i ^ bits) for i in range(columns)])]
    ppermute x15 -> x10, starting transfers between devices: 14.6 us -> 11.8 us  [exchange(): return lax.ppermute(array, 'col', [(i, i ^ bits) for i in range(columns)])]
    ppermute x1, waiting for transfers between devices: 6.7 us -> 6.04 us  [local(): lax.ppermute(sent[n - 1], 'row', [(i, (i + n) % regions) for i in range(r...]
    add x2 -> x0, other arithmetic: 0.64 us -> none  [the longest x1 0.63 us: local(): code = source * 65536 + target + place // pairs * (regions * lanes)]
    unnamed x42 -> x2, local copies, waits for them, and re-layouts: 1.45 us -> 0.95 us
  transfers between devices with their start and end apart: 16 -> 11, of which waited for: 6 -> 5; matrix products, arithmetic and copies ran while one was open for 1% -> 0% of each run, Pallas kernels for 8% -> 9%
where the time goes in v2:
time: 38 us; the launch traced here: 37.8 us
  waiting for transfers between devices  17.4 us (46%)
  starting transfers between devices  13.3 us (35%)
  Pallas kernels  6.05 us (16%)
  local copies, waits for them, and re-layouts  0.95 us (2%)
    ppermute x10, starting transfers between devices, exchange(): return lax.ppermute(array, 'col', [(i, i ^ bits) for i in range(columns)])  11.8 us
    ppermute x10, waiting for transfers between devices, exchange(): return lax.ppermute(array, 'col', [(i, i ^ bits) for i in range(columns)])  11.4 us
    ppermute x1, waiting for transfers between devices, local(): lax.ppermute(sent[n - 1], 'row', [(i, (i + n) % regions) for i in range(r...  6.04 us
    pallas_call x1, Pallas kernels, local(): call(left_kernel, (pltpu.VMEM((rows * entries, order, order), jnp.bfloat1...  3.48 us
    ppermute x1, starting transfers between devices, local(): lax.ppermute(sent[n - 1], 'row', [(i, (i + n) % regions) for i in range(r...  1.57 us
    pallas_call x1, Pallas kernels, local(): call(sum_kernel, (pltpu.VMEM((half, order, width), jnp.float32), pltpu.VM...  1.5 us
    unnamed x2, local copies, waits for them, and re-layouts  0.95 us
    pallas_call x1, Pallas kernels, local(): call(add_kernel, jax.ShapeDtypeStruct((lanes, order, order), jnp.bfloat16...  0.9 us
  transfers between devices with their start and end apart: 11, of which 5 were waited for; matrix products, arithmetic and copies ran while one was open for 0% of the time, Pallas kernels for 9%

profile of v2, /device:TPU:0, one launch (start us, length us, event | category | flops | bytes accessed | tf_op | source)
XLA Modules:
  0.0 37.8 jit_solution(11374915598339480590)
XLA Ops:
  0.0 0.0 copy-start
  0.0 0.9 %copy-done = bf16[16,64,64]{2,1,0:T(8,128)(2,1)S(1)} copy-done((bf16[16,64,64]{2,1,0:T(8,128)(2,1)S(1)}, bf16[16,64,64]{2,1,0:T(8,128)(2,1)}, u32[]{:S(2)}) %copy-start) | copy-done | bytes 131096
  1.0 0.1 shard_map.73
  1.1 5.1 %collective-permute-start.2 = (bf16[8,64,128]{2,1,0:T(8,128)(2,1)S(1)}, bf16[8,64,128]{2,1,0:T(8,128)(2,1)S(1)}, u32[]{:S(2)}, u32[]{:S(2)}) collective-permute-start(bf16[8,64,128]{2,1,0:T(8,128)(2,1)S(1)} %get-tuple-element.14.refs_0_), channel_id=1, source_target_pairs={{0,12},{1,13},{2,14},{3,15},{4,8},{5,9},{6,10},{7,11},{8,4},{9,5},... | collective-permute-start | bytes 393224 | tf_op jit(solution)/shard_map/ppermute | solution.py:160
  6.2 0.0 collective-permute-start.1
  6.2 1.5 %collective-permute-start = (bf16[8,64,128]{2,1,0:T(8,128)(2,1)S(1)}, bf16[8,64,128]{2,1,0:T(8,128)(2,1)S(1)}, u32[]{:S(2)}, u32[]{:S(2)}) collective-permute-start(bf16[8,64,128]{2,1,0:T(8,128)(2,1)S(1)} %get-tuple-element.14.refs_0_), channel_id=1, source_target_pairs={{0,2},{1,3},{2,0},{3,1},{4,6},{5,7},{6,4},{7,5},{8,10},{9,11},{10,... | collective-permute-start | bytes 393224 | tf_op jit(solution)/shard_map/ppermute | solution.py:160
  7.7 2.9 %collective-permute-done.2.refs_3_ = bf16[8,64,128]{2,1,0:T(8,128)(2,1)S(1)} collective-permute-done((bf16[8,64,128]{2,1,0:T(8,128)(2,1)S(1)}, bf16[8,64,128]{2,1,0:T(8,128)(2,1)S(1)}, u32[]{:S(2)}, u32[]{:S(2)}) %collective-permute-start.2) | collective-permute-done | bytes 131104 | tf_op jit(solution)/shard_map/ppermute | solution.py:160
  10.6 2.0 %collective-permute-done.1.refs_2_ = bf16[8,64,128]{2,1,0:T(8,128)(2,1)S(1)} collective-permute-done((bf16[8,64,128]{2,1,0:T(8,128)(2,1)S(1)}, bf16[8,64,128]{2,1,0:T(8,128)(2,1)S(1)}, u32[]{:S(2)}, u32[]{:S(2)}) %collective-permute-start.1) | collective-permute-done | bytes 131104 | tf_op jit(solution)/shard_map/ppermute | solution.py:160
  12.6 0.0 collective-permute-done.refs_1_
  12.7 0.1 collective-permute-start.3
  12.7 1.6 %collective-permute-start.5 = (bf16[8,64,128]{2,1,0:T(8,128)(2,1)S(1)}, bf16[8,64,128]{2,1,0:T(8,128)(2,1)S(1)}, u32[]{:S(2)}, u32[]{:S(2)}) collective-permute-start(bf16[8,64,128]{2,1,0:T(8,128)(2,1)S(1)} %collective-permute-done.1.refs_2_), channel_id=1, source_target_pairs={{0,2},{1,3},{2,0},{3,1},{4,6},{5,7},{6,4},{7,5},{8,10},{9,11},{10,... | collective-permute-start | bytes 393224 | tf_op jit(solution)/shard_map/ppermute | solution.py:160
  14.3 0.5 %collective-permute-start.4 = (bf16[8,64,128]{2,1,0:T(8,128)(2,1)S(1)}, bf16[8,64,128]{2,1,0:T(8,128)(2,1)S(1)}, u32[]{:S(2)}, u32[]{:S(2)}) collective-permute-start(bf16[8,64,128]{2,1,0:T(8,128)(2,1)S(1)} %collective-permute-done.refs_1_), channel_id=1, source_target_pairs={{0,8},{1,9},{2,10},{3,11},{4,12},{5,13},{6,14},{7,15},{8,0},{9,1},... | collective-permute-start | bytes 393224 | tf_op jit(solution)/shard_map/ppermute | solution.py:160
  14.8 0.5 %collective-permute-start.8 = (bf16[8,64,128]{2,1,0:T(8,128)(2,1)S(1)}, bf16[8,64,128]{2,1,0:T(8,128)(2,1)S(1)}, u32[]{:S(2)}, u32[]{:S(2)}) collective-permute-start(bf16[8,64,128]{2,1,0:T(8,128)(2,1)S(1)} %collective-permute-done.2.refs_3_), channel_id=1, source_target_pairs={{0,2},{1,3},{2,0},{3,1},{4,6},{5,7},{6,4},{7,5},{8,10},{9,11},{10,... | collective-permute-start | bytes 393224 | tf_op jit(solution)/shard_map/ppermute | solution.py:160
  15.3 1.8 %collective-permute-start.7 = (bf16[8,64,128]{2,1,0:T(8,128)(2,1)S(1)}, bf16[8,64,128]{2,1,0:T(8,128)(2,1)S(1)}, u32[]{:S(2)}, u32[]{:S(2)}) collective-permute-start(bf16[8,64,128]{2,1,0:T(8,128)(2,1)S(1)} %collective-permute-done.2.refs_3_), channel_id=1, source_target_pairs={{0,4},{1,5},{2,6},{3,7},{4,0},{5,1},{6,2},{7,3},{8,12},{9,13},{10,... | collective-permute-start | bytes 393224 | tf_op jit(solution)/shard_map/ppermute | solution.py:160
  17.2 2.0 %collective-permute-done.5.refs_1_ = bf16[8,64,128]{2,1,0:T(8,128)(2,1)S(1)} collective-permute-done((bf16[8,64,128]{2,1,0:T(8,128)(2,1)S(1)}, bf16[8,64,128]{2,1,0:T(8,128)(2,1)S(1)}, u32[]{:S(2)}, u32[]{:S(2)}) %collective-permute-start.5) | collective-permute-done | bytes 131104 | tf_op jit(solution)/shard_map/ppermute | solution.py:160
  19.2 4.5 %collective-permute-done.4.refs_0_ = bf16[8,64,128]{2,1,0:T(8,128)(2,1)S(1)} collective-permute-done((bf16[8,64,128]{2,1,0:T(8,128)(2,1)S(1)}, bf16[8,64,128]{2,1,0:T(8,128)(2,1)S(1)}, u32[]{:S(2)}, u32[]{:S(2)}) %collective-permute-start.4) | collective-permute-done | bytes 131104 | tf_op jit(solution)/shard_map/ppermute | solution.py:160
  23.6 0.1 collective-permute-start.6
  23.7 0.0 collective-permute-done.8.refs_1_
  23.7 0.0 collective-permute-done.7.refs_0_
  23.8 0.5 %collective-permute-start.9 = (bf16[16,64,128]{2,1,0:T(8,128)(2,1)S(1)}, bf16[16,64,128]{2,1,0:T(8,128)(2,1)S(1)}, u32[]{:S(2)}, u32[]{:S(2)}) collective-permute-start(bf16[16,64,128]{2,1,0:T(8,128)(2,1)S(1)} %shard_map.77.refs_4_), channel_id=1, source_target_pairs={{0,1},{1,0},{2,3},{3,2},{4,5},{5,4},{6,7},{7,6},{8,9},{9,8},{10,11... | collective-permute-start | bytes 786440 | tf_op jit(solution)/shard_map/ppermute | solution.py:160
  24.3 3.5 %shard_map.74 = (bf16[112,64,64]{2,1,0:T(8,128)(2,1)S(1)}, s32[7,16]{1,0:T(8,128)S(4)}) custom-call(bf16[16,64,64]{2,1,0:T(8,128)(2,1)S(1)} %get-tuple-element.11.p_ref, bf16[16,7,64,64]{3,2,1,0:T(8,128)(2,1)} %a_ref.1, s32[7,16]{1,0:T(8,128)} %bitcast.8, s32[7,16]{1,0:T(8,128)} %bitcast.9, s32[1,16]{1,0:T(1,128)} %bitcast.11, s32[7,16]{1,0:T(8,128)} %bitcast.10, ...), custom_call_target="tpu_custom_call" | custom-call | tf_op jit(solution)/shard_map/pallas_call | solution.py:184
  27.8 0.0 collective-permute-done.6.refs_3_
  27.8 0.0 collective-permute-done.9.refs_5_
  27.8 0.0 collective-permute-done.3.refs_1_
  27.8 1.5 %shard_map.78 = (f32[14,64,128]{2,1,0:T(8,128)S(1)}, bf16[1,14,64,128]{3,2,1,0:T(8,128)(2,1)S(1)}) custom-call(s32[7,16]{1,0:T(8,128)S(4)} %get-tuple-element.12.code_ref, bf16[112,64,64]{2,1,0:T(8,128)(2,1)S(1)} %get-tuple-element.13.x_ref, bf16[32,64,128]{2,1,0:T(8,128)(2,1)S(1)} %shard_map.75.refs_0_, ...), custom_call_target="tpu_custom_call" | custom-call | tf_op jit(solution)/shard_map/pallas_call | solution.py:203
  29.3 1.6 %collective-permute-start.10 = (bf16[14,64,128]{2,1,0:T(8,128)(2,1)S(1)}, bf16[14,64,128]{2,1,0:T(8,128)(2,1)S(1)}, u32[]{:S(2)}, u32[]{:S(2)}) collective-permute-start(bf16[14,64,128]{2,1,0:T(8,128)(2,1)S(1)} %bitcast.7), channel_id=1, source_target_pairs={{0,16},{16,0},{1,17},{17,1},{2,18},{18,2},{3,19},{19,3},{4,20},{20... | collective-permute-start | bytes 688136 | tf_op jit(solution)/shard_map/ppermute | solution.py:218
  30.9 6.0 %collective-permute-done.10.refs_0_ = bf16[14,64,128]{2,1,0:T(8,128)(2,1)S(1)} collective-permute-done((bf16[14,64,128]{2,1,0:T(8,128)(2,1)S(1)}, bf16[14,64,128]{2,1,0:T(8,128)(2,1)S(1)}, u32[]{:S(2)}, u32[]{:S(2)}) %collective-permute-start.10) | collective-permute-done | bytes 229408 | tf_op jit(solution)/shard_map/ppermute | solution.py:218
  36.9 0.9 %shard_map.79 = bf16[28,64,64]{2,1,0:T(8,128)(2,1)} custom-call(f32[14,64,128]{2,1,0:T(8,128)S(1)} %get-tuple-element.15.own_ref, bf16[14,64,128]{2,1,0:T(8,128)(2,1)S(1)} %collective-permute-done.10.refs_0_), custom_call_target="tpu_custom_call" | custom-call | tf_op jit(solution)/shard_map/pallas_call | solution.py:221
  (3 shorter events, 0.1 us)
Async XLA Ops:
  0.0 0.9 %copy-start = (bf16[16,64,64]{2,1,0:T(8,128)(2,1)S(1)}, bf16[16,64,64]{2,1,0:T(8,128)(2,1)}, u32[]{:S(2)}) copy-start(bf16[16,64,64]{2,1,0:T(8,128)(2,1)} %p_ref.1) | copy-start | bytes 393220
  1.1 9.5 %collective-permute-start.2 = (bf16[8,64,128]{2,1,0:T(8,128)(2,1)S(1)}, bf16[8,64,128]{2,1,0:T(8,128)(2,1)S(1)}, u32[]{:S(2)}, u32[]{:S(2)}) collective-permute-start(bf16[8,64,128]{2,1,0:T(8,128)(2,1)S(1)} %get-tuple-element.14.refs_0_), channel_id=1, source_target_pairs={{0,12},{1,13},{2,14},{3,15},{4,8},{5,9},{6,10},{7,11},{8,4},{9,5},... | collective-permute-start | bytes 393224 | tf_op jit(solution)/shard_map/ppermute | solution.py:160
  6.2 6.4 %collective-permute-start.1 = (bf16[8,64,128]{2,1,0:T(8,128)(2,1)S(1)}, bf16[8,64,128]{2,1,0:T(8,128)(2,1)S(1)}, u32[]{:S(2)}, u32[]{:S(2)}) collective-permute-start(bf16[8,64,128]{2,1,0:T(8,128)(2,1)S(1)} %get-tuple-element.14.refs_0_), channel_id=1, source_target_pairs={{0,4},{1,5},{2,6},{3,7},{4,0},{5,1},{6,2},{7,3},{8,12},{9,13},{10,... | collective-permute-start | bytes 393224 | tf_op jit(solution)/shard_map/ppermute | solution.py:160
  6.2 6.4 %collective-permute-start = (bf16[8,64,128]{2,1,0:T(8,128)(2,1)S(1)}, bf16[8,64,128]{2,1,0:T(8,128)(2,1)S(1)}, u32[]{:S(2)}, u32[]{:S(2)}) collective-permute-start(bf16[8,64,128]{2,1,0:T(8,128)(2,1)S(1)} %get-tuple-element.14.refs_0_), channel_id=1, source_target_pairs={{0,2},{1,3},{2,0},{3,1},{4,6},{5,7},{6,4},{7,5},{8,10},{9,11},{10,... | collective-permute-start | bytes 393224 | tf_op jit(solution)/shard_map/ppermute | solution.py:160
  12.7 15.2 %collective-permute-start.3 = (bf16[32,64,128]{2,1,0:T(8,128)(2,1)S(1)}, bf16[32,64,128]{2,1,0:T(8,128)(2,1)S(1)}, u32[]{:S(2)}, u32[]{:S(2)}) collective-permute-start(bf16[32,64,128]{2,1,0:T(8,128)(2,1)S(1)} %shard_map.75.refs_0_), channel_id=1, source_target_pairs={{0,1},{1,0},{2,3},{3,2},{4,5},{5,4},{6,7},{7,6},{8,9},{9,8},{10,11... | collective-permute-start | bytes 1572872 | tf_op jit(solution)/shard_map/ppermute | solution.py:160
  12.7 6.4 %collective-permute-start.5 = (bf16[8,64,128]{2,1,0:T(8,128)(2,1)S(1)}, bf16[8,64,128]{2,1,0:T(8,128)(2,1)S(1)}, u32[]{:S(2)}, u32[]{:S(2)}) collective-permute-start(bf16[8,64,128]{2,1,0:T(8,128)(2,1)S(1)} %collective-permute-done.1.refs_2_), channel_id=1, source_target_pairs={{0,2},{1,3},{2,0},{3,1},{4,6},{5,7},{6,4},{7,5},{8,10},{9,11},{10,... | collective-permute-start | bytes 393224 | tf_op jit(solution)/shard_map/ppermute | solution.py:160
  14.3 9.3 %collective-permute-start.4 = (bf16[8,64,128]{2,1,0:T(8,128)(2,1)S(1)}, bf16[8,64,128]{2,1,0:T(8,128)(2,1)S(1)}, u32[]{:S(2)}, u32[]{:S(2)}) collective-permute-start(bf16[8,64,128]{2,1,0:T(8,128)(2,1)S(1)} %collective-permute-done.refs_1_), channel_id=1, source_target_pairs={{0,8},{1,9},{2,10},{3,11},{4,12},{5,13},{6,14},{7,15},{8,0},{9,1},... | collective-permute-start | bytes 393224 | tf_op jit(solution)/shard_map/ppermute | solution.py:160
  14.8 8.9 %collective-permute-start.8 = (bf16[8,64,128]{2,1,0:T(8,128)(2,1)S(1)}, bf16[8,64,128]{2,1,0:T(8,128)(2,1)S(1)}, u32[]{:S(2)}, u32[]{:S(2)}) collective-permute-start(bf16[8,64,128]{2,1,0:T(8,128)(2,1)S(1)} %collective-permute-done.2.refs_3_), channel_id=1, source_target_pairs={{0,2},{1,3},{2,0},{3,1},{4,6},{5,7},{6,4},{7,5},{8,10},{9,11},{10,... | collective-permute-start | bytes 393224 | tf_op jit(solution)/shard_map/ppermute | solution.py:160
  15.3 8.4 %collective-permute-start.7 = (bf16[8,64,128]{2,1,0:T(8,128)(2,1)S(1)}, bf16[8,64,128]{2,1,0:T(8,128)(2,1)S(1)}, u32[]{:S(2)}, u32[]{:S(2)}) collective-permute-start(bf16[8,64,128]{2,1,0:T(8,128)(2,1)S(1)} %collective-permute-done.2.refs_3_), channel_id=1, source_target_pairs={{0,4},{1,5},{2,6},{3,7},{4,0},{5,1},{6,2},{7,3},{8,12},{9,13},{10,... | collective-permute-start | bytes 393224 | tf_op jit(solution)/shard_map/ppermute | solution.py:160
  23.6 4.2 %collective-permute-start.6 = (bf16[16,64,128]{2,1,0:T(8,128)(2,1)S(1)}, bf16[16,64,128]{2,1,0:T(8,128)(2,1)S(1)}, u32[]{:S(2)}, u32[]{:S(2)}) collective-permute-start(bf16[16,64,128]{2,1,0:T(8,128)(2,1)S(1)} %shard_map.76.refs_2_), channel_id=1, source_target_pairs={{0,1},{1,0},{2,3},{3,2},{4,5},{5,4},{6,7},{7,6},{8,9},{9,8},{10,11... | collective-permute-start | bytes 786440 | tf_op jit(solution)/shard_map/ppermute | solution.py:160
  23.8 4.0 %collective-permute-start.9 = (bf16[16,64,128]{2,1,0:T(8,128)(2,1)S(1)}, bf16[16,64,128]{2,1,0:T(8,128)(2,1)S(1)}, u32[]{:S(2)}, u32[]{:S(2)}) collective-permute-start(bf16[16,64,128]{2,1,0:T(8,128)(2,1)S(1)} %shard_map.77.refs_4_), channel_id=1, source_target_pairs={{0,1},{1,0},{2,3},{3,2},{4,5},{5,4},{6,7},{7,6},{8,9},{9,8},{10,11... | collective-permute-start | bytes 786440 | tf_op jit(solution)/shard_map/ppermute | solution.py:160
  29.3 7.6 %collective-permute-start.10 = (bf16[14,64,128]{2,1,0:T(8,128)(2,1)S(1)}, bf16[14,64,128]{2,1,0:T(8,128)(2,1)S(1)}, u32[]{:S(2)}, u32[]{:S(2)}) collective-permute-start(bf16[14,64,128]{2,1,0:T(8,128)(2,1)S(1)} %bitcast.7), channel_id=1, source_target_pairs={{0,16},{16,0},{1,17},{17,1},{2,18},{18,2},{3,19},{19,3},{4,20},{20... | collective-permute-start | bytes 688136 | tf_op jit(solution)/shard_map/ppermute | solution.py:218

commit v3 on v2

--- a/solution.py
+++ b/solution.py
@@ -1,3 +1,5 @@
+import functools
+
 import jax
 import jax.numpy as jnp
 from jax import lax
@@ -11,7 +13,7 @@
 SMEM = pl.BlockSpec(memory_space=pltpu.SMEM)
 HBM = pl.BlockSpec(memory_space=pltpu.HBM)
 LIMIT = 1 << 20
-PARTS = 8
+PARTS = 2
 
 
 def keep(*arrays):
@@ -19,11 +21,11 @@
 
 
 def routes(columns):
-    near = {4: 0, 12: 0, 2: 0, 6: 4, 10: 2, 8: 12, 14: 12}
+    near = {12: 0, 2: 0, 4: 0, 10: 2, 8: 12, 14: 12, 6: 4}
     order = [key for key in near if key < columns]
     far = list(range(16, columns, 2))
     parents = {key: near[key] for key in order} | {key: key & 15 for key in far}
-    groups = [[0, 2, 4, 12], [10, 6], [8, 14], far]
+    groups = [[0, 2, 4, 12], [10, 8, 14], [6], far]
     groups = [[key for key in group if key < columns] for group in groups]
     return order + far, parents, [group for group in groups if group]
 
@@ -65,29 +67,44 @@
     return source * 65536 + target + high * (regions * lanes)
 
 
-def left_kernel(p_ref, a_ref, peer_ref, place_ref, owner_ref, slot_ref, row_ref, x_ref, out_ref, *held):
-    *index_held, a_held, code_ref, index_sems, sems, code_sem = held
+def visits(owner_ref):
+    region, rows = lax.axis_index("row"), owner_ref.shape[1]
+    column = lax.broadcasted_iota(jnp.int32, (rows, rows), 1)
+    row = lax.broadcasted_iota(jnp.int32, (rows, rows), 0)
+    away = jnp.where(owner_ref[...] != region, 1, 0) + jnp.zeros((rows, rows), jnp.int32)
+    mine = jnp.sum(jnp.where(column == row, away, 0), axis=1, keepdims=True)
+    before = jnp.sum(jnp.where(column < row, away, 0), axis=1, keepdims=True)
+    total = jnp.sum(away, axis=1, keepdims=True)
+    number = lax.broadcasted_iota(jnp.int32, (rows, 1), 0)
+    place = jnp.where(mine > 0, before, total + number - before)
+    return jnp.sum(jnp.where(place == column, row, 0), axis=0, keepdims=True)
+
+
+def code_kernel(*refs):
+    sources, (out_ref, *held, code_ref, sems) = refs[:5], refs[5:]
+    copies = [
+        pltpu.make_async_copy(source, target, sems.at[n])
+        for n, (source, target) in enumerate(zip(sources, held))
+    ]
+    for copy in copies:
+        copy.start()
+    for copy in copies:
+        copy.wait()
+    entries = held[0].shape[0]
+    code_ref[:entries] = codes(*held)
+    code_ref[entries:] = visits(held[2])
+    pltpu.sync_copy(code_ref, out_ref)
+
+
+def left_kernel(p_ref, a_ref, x_ref, a_held, sems):
     rows, entries = a_ref.shape[:2]
     parts = sems.shape[0]
     step = rows // parts
-    index_copies = [
-        pltpu.make_async_copy(source, target, index_sems.at[n])
-        for n, (source, target) in enumerate(
-            zip((peer_ref, place_ref, owner_ref, slot_ref, row_ref), index_held)
-        )
-    ]
-    for copy in index_copies:
-        copy.start()
     copies = []
     for n in range(parts):
         part = pl.ds(n * step, step)
         copies.append(pltpu.make_async_copy(a_ref.at[part], a_held.at[part], sems.at[n]))
         copies[n].start()
-    for copy in index_copies:
-        copy.wait()
-    code_ref[...] = codes(*index_held)
-    code_copy = pltpu.make_async_copy(code_ref, out_ref, code_sem)
-    code_copy.start()
     for n in range(parts):
         copies[n].wait()
         for i in range(n * step, (n + 1) * step):
@@ -97,7 +114,6 @@
                     preferred_element_type=jnp.float32,
                 )
                 x_ref[i * entries + k] = x.astype(x_ref.dtype)
-    code_copy.wait()
 
 
 def fold(acc_ref, base, half, j, low):
@@ -108,27 +124,50 @@
     return first + pltpu.roll(second, order, axis=1)
 
 
-def sum_kernel(code_ref, x_ref, *refs):
-    *pieces, own_ref, sent_ref, gathered_ref, acc_ref = refs
-    entries, rows = code_ref.shape
-    order, width = pieces[0].shape[1:]
+def accumulate(visited, code_ref, x_ref, gathered_ref, acc_ref):
+    entries = code_ref.shape[0] - 1
+    for i in visited:
+        row = code_ref[entries, i]
+        for k in range(entries):
+            code = code_ref[k, row]
+            source, target = code >> 16, code & 0xFFFF
+            acc_ref[target] += jnp.dot(
+                x_ref[row * entries + k], gathered_ref[source], preferred_element_type=jnp.float32
+            )
+
+
+def lower_half(order, width):
+    return lax.broadcasted_iota(jnp.int32, (order, width), 1) < width // 2
+
+
+def ready_kernel(*refs):
+    *pieces, acc_ref, gathered_ref = refs
     acc_ref[...] = jnp.zeros_like(acc_ref)
     merge_kernel(*pieces, gathered_ref)
-    for i in range(rows):
-        for k in range(entries):
-            code = code_ref[k, i]
-            source, target = code >> 16, code & 0xFFFF
-            acc_ref[target] += jnp.dot(
-                x_ref[i * entries + k], gathered_ref[source], preferred_element_type=jnp.float32
-            )
-    lanes = lax.broadcasted_iota(jnp.int32, (order, width), 1)
-    low = lanes < width // 2
-    half = own_ref.shape[0]
+
+
+def away_kernel(visits, code_ref, x_ref, acc_in_ref, gathered_in_ref, *refs):
+    *pieces, sent_ref, acc_ref, gathered_ref = refs
+    regions, half, order, width = sent_ref.shape
+    start = gathered_ref.shape[0] - sum(piece.shape[0] for piece in pieces)
+    merge_kernel(*pieces, gathered_ref.at[start:])
+    accumulate(range(visits), code_ref, x_ref, gathered_ref, acc_ref)
+    low = lower_half(order, width)
+    for n in range(regions):
+        for j in range(half):
+            sent_ref[n, j] = fold(acc_ref, 2 * half * (n + 1), half, j, low).astype(sent_ref.dtype)
+
+
+def home_kernel(visits, code_ref, x_ref, gathered_ref, acc_in_ref, own_ref, acc_ref):
+    half, order, width = own_ref.shape
+    rows = code_ref.shape[1]
+    total = acc_ref.shape[0] // 2
+    for n in range(2):
+        acc_ref[n * total : n * total + 2 * half] = acc_in_ref[n * total : n * total + 2 * half]
+    accumulate(range(visits, rows), code_ref, x_ref, gathered_ref, acc_ref)
+    low = lower_half(order, width)
     for j in range(half):
         own_ref[j] = fold(acc_ref, 0, half, j, low)
-    for n in range(sent_ref.shape[0]):
-        for j in range(half):
-            sent_ref[n, j] = fold(acc_ref, 2 * half * (n + 1), half, j, low).astype(sent_ref.dtype)
 
 
 def add_kernel(own_ref, *refs):
@@ -142,10 +181,10 @@
         out_ref[half + j] = pltpu.roll(total, width // 2, axis=1)[:, : width // 2].astype(out_ref.dtype)
 
 
-def call(kernel, out_shape, in_specs, out_specs, scratch_shapes=(), limit=LIMIT):
+def call(kernel, out_shape, in_specs, out_specs, scratch_shapes=(), limit=LIMIT, aliases=None):
     return pl.pallas_call(
         kernel, out_shape=out_shape, in_specs=in_specs, out_specs=out_specs,
-        scratch_shapes=scratch_shapes,
+        scratch_shapes=scratch_shapes, input_output_aliases=aliases or {},
         compiler_params=pltpu.CompilerParams(vmem_limit_bytes=limit),
     )
 
@@ -180,44 +219,50 @@
         )(*keep(*[held[key] for key in group]))
         pieces += [mine, exchange(mine, 1)]
 
+    x = call(
+        left_kernel, pltpu.VMEM((rows * entries, order, order), jnp.bfloat16),
+        [VMEM, HBM], VMEM,
+        [pltpu.VMEM(a_blocks.shape, a_blocks.dtype), pltpu.SemaphoreType.DMA((PARTS,))],
+        limit=a_blocks.size * 4 + LIMIT,
+    )(*keep(kept), pltpu.with_memory_space_constraint(a_blocks, pltpu.HBM))
     indices = (a_peer.T, a_local.T, agg_owner.T, entry_slot.T, agg_local[None])
-    x, code = call(
-        left_kernel,
-        (
-            pltpu.VMEM((rows * entries, order, order), jnp.bfloat16),
-            pltpu.SMEM((entries, rows), jnp.int32),
-        ),
-        [VMEM] + [HBM] * 6, (VMEM, SMEM),
+    code = call(
+        code_kernel, pltpu.SMEM((entries + 1, rows), jnp.int32), [HBM] * 5, SMEM,
         [pltpu.VMEM(array.shape, array.dtype) for array in indices]
-        + [
-            pltpu.VMEM(a_blocks.shape, a_blocks.dtype), pltpu.VMEM((entries, rows), jnp.int32),
-            pltpu.SemaphoreType.DMA((len(indices),)), pltpu.SemaphoreType.DMA((PARTS,)),
-            pltpu.SemaphoreType.DMA(()),
-        ],
-        limit=a_blocks.size * 4 + LIMIT,
-    )(*keep(kept), *[pltpu.with_memory_space_constraint(v, pltpu.HBM) for v in (a_blocks, *indices)])
+        + [pltpu.VMEM((entries + 1, rows), jnp.int32), pltpu.SemaphoreType.DMA((5,))],
+    )(*[pltpu.with_memory_space_constraint(array, pltpu.HBM) for array in indices])
 
     half = lanes // 2
     width = 2 * order
-    scratch = (columns * pairs * 2 + 2 * regions * lanes * 4) * order * width
-    own_sum, sent = call(
-        sum_kernel,
+    acc = (2 * regions * lanes, order, width)
+    most = -(-rows // regions) + 1
+    visits_away = min(rows, (regions - 1) * most)
+    code = pltpu.with_memory_space_constraint(code, pltpu.SMEM)
+    sums, gathered = call(
+        ready_kernel,
+        (pltpu.VMEM(acc, jnp.float32), pltpu.VMEM((columns * pairs, order, width), p_blocks.dtype)),
+        [VMEM] * 2, (VMEM, VMEM),
+    )(*keep(*pieces[:2]))
+    sent, sums, gathered = call(
+        functools.partial(away_kernel, visits_away),
         (
-            pltpu.VMEM((half, order, width), jnp.float32),
             pltpu.VMEM((regions - 1, half, order, width), jnp.bfloat16),
+            pltpu.VMEM(acc, jnp.float32),
+            pltpu.VMEM((columns * pairs, order, width), p_blocks.dtype),
         ),
-        [SMEM] + [VMEM] * (1 + len(pieces)), (VMEM, VMEM),
-        [
-            pltpu.VMEM((columns * pairs, order, width), p_blocks.dtype),
-            pltpu.VMEM((2 * regions * lanes, order, width), jnp.float32),
-        ],
-        limit=scratch + LIMIT,
-    )(pltpu.with_memory_space_constraint(code, pltpu.SMEM), *keep(x, *pieces))
+        [SMEM] + [VMEM] * (1 + len(pieces)), (VMEM, VMEM, VMEM), aliases={2: 1, 3: 2},
+    )(code, *keep(x, sums, gathered, *pieces[2:]))
 
     received = [
         lax.ppermute(sent[n - 1], "row", [(i, (i + n) % regions) for i in range(regions)])
         for n in range(1, regions)
     ]
+    own_sum = call(
+        functools.partial(home_kernel, visits_away),
+        pltpu.VMEM((half, order, width), jnp.float32),
+        [SMEM] + [VMEM] * 3, VMEM, [pltpu.VMEM(acc, jnp.float32)],
+        limit=acc[0] * order * width * 4 + LIMIT,
+    )(code, *keep(x, gathered, sums))
     out = call(
         add_kernel, jax.ShapeDtypeStruct((lanes, order, order), jnp.bfloat16),
         [VMEM] * regions, VMEM, limit=4 << 20,

time: 38 us -> 44.9 us (1.18)
  waiting for transfers between devices: 17.4 us -> 24.2 us
    ppermute x10, waiting for transfers between devices: 11.4 us -> 18.5 us  [exchange(): return lax.ppermute(array, 'col', [(i, i ^ bits) for i in range(columns)])]
    pallas_call x2 -> x5, Pallas kernels: 4.98 us -> 5.41 us  [the longest x1 2.1 us: local(): call(left_kernel, pltpu.VMEM((rows * entries, order, order), jnp.bfloat16...]
  transfers between devices with their start and end apart: 11 -> 11, of which waited for: 5 -> 7; matrix products, arithmetic and copies ran while one was open for 0% -> 0% of each run, Pallas kernels for 9% -> 10%
where the time goes in v3:
time: 44.9 us; the launch traced here: 44.7 us
  waiting for transfers between devices  24.2 us (54%)
  starting transfers between devices  12.9 us (29%)
  Pallas kernels  6.48 us (14%)
  local copies, waits for them, and re-layouts  0.95 us (2%)
    ppermute x10, waiting for transfers between devices, exchange(): return lax.ppermute(array, 'col', [(i, i ^ bits) for i in range(columns)])  18.5 us
    ppermute x10, starting transfers between devices, exchange(): return lax.ppermute(array, 'col', [(i, i ^ bits) for i in range(columns)])  11.4 us
    ppermute x1, waiting for transfers between devices, local(): lax.ppermute(sent[n - 1], 'row', [(i, (i + n) % regions) for i in range(r...  5.77 us
    pallas_call x1, Pallas kernels, local(): call(left_kernel, pltpu.VMEM((rows * entries, order, order), jnp.bfloat16...  2.1 us
    ppermute x1, starting transfers between devices, local(): lax.ppermute(sent[n - 1], 'row', [(i, (i + n) % regions) for i in range(r...  1.56 us
    pallas_call x1, Pallas kernels, local(): call(code_kernel, pltpu.SMEM((entries + 1, rows), jnp.int32), [HBM] * 5,...  1.49 us
    unnamed x2, local copies, waits for them, and re-layouts  0.95 us
    pallas_call x1, Pallas kernels, local(): call(add_kernel, jax.ShapeDtypeStruct((lanes, order, order), jnp.bfloat16...  0.9 us
  transfers between devices with their start and end apart: 11, of which 7 were waited for; matrix products, arithmetic and copies ran while one was open for 0% of the time, Pallas kernels for 10%

profile of v3, /device:TPU:0, one launch (start us, length us, event | category | flops | bytes accessed | tf_op | source)
XLA Modules:
  0.0 44.7 jit_solution(14840299131724371504)
XLA Ops:
  0.0 0.0 copy-start
  0.0 0.9 %copy-done = bf16[16,64,64]{2,1,0:T(8,128)(2,1)S(1)} copy-done((bf16[16,64,64]{2,1,0:T(8,128)(2,1)S(1)}, bf16[16,64,64]{2,1,0:T(8,128)(2,1)}, u32[]{:S(2)}) %copy-start) | copy-done | bytes 131096
  1.0 0.1 shard_map.74
  1.1 5.1 %collective-permute-start.2 = (bf16[8,64,128]{2,1,0:T(8,128)(2,1)S(1)}, bf16[8,64,128]{2,1,0:T(8,128)(2,1)S(1)}, u32[]{:S(2)}, u32[]{:S(2)}) collective-permute-start(bf16[8,64,128]{2,1,0:T(8,128)(2,1)S(1)} %get-tuple-element.13.refs_0_), channel_id=1, source_target_pairs={{0,12},{1,13},{2,14},{3,15},{4,8},{5,9},{6,10},{7,11},{8,4},{9,5},... | collective-permute-start | bytes 393224 | tf_op jit(solution)/shard_map/ppermute | solution.py:199
  6.2 0.0 collective-permute-start.1
  6.2 1.5 %collective-permute-start = (bf16[8,64,128]{2,1,0:T(8,128)(2,1)S(1)}, bf16[8,64,128]{2,1,0:T(8,128)(2,1)S(1)}, u32[]{:S(2)}, u32[]{:S(2)}) collective-permute-start(bf16[8,64,128]{2,1,0:T(8,128)(2,1)S(1)} %get-tuple-element.13.refs_0_), channel_id=1, source_target_pairs={{0,2},{1,3},{2,0},{3,1},{4,6},{5,7},{6,4},{7,5},{8,10},{9,11},{10,... | collective-permute-start | bytes 393224 | tf_op jit(solution)/shard_map/ppermute | solution.py:199
  7.7 2.9 %collective-permute-done.2.refs_3_ = bf16[8,64,128]{2,1,0:T(8,128)(2,1)S(1)} collective-permute-done((bf16[8,64,128]{2,1,0:T(8,128)(2,1)S(1)}, bf16[8,64,128]{2,1,0:T(8,128)(2,1)S(1)}, u32[]{:S(2)}, u32[]{:S(2)}) %collective-permute-start.2) | collective-permute-done | bytes 131104 | tf_op jit(solution)/shard_map/ppermute | solution.py:199
  10.6 2.0 %collective-permute-done.1.refs_2_ = bf16[8,64,128]{2,1,0:T(8,128)(2,1)S(1)} collective-permute-done((bf16[8,64,128]{2,1,0:T(8,128)(2,1)S(1)}, bf16[8,64,128]{2,1,0:T(8,128)(2,1)S(1)}, u32[]{:S(2)}, u32[]{:S(2)}) %collective-permute-start.1) | collective-permute-done | bytes 131104 | tf_op jit(solution)/shard_map/ppermute | solution.py:199
  12.6 0.0 collective-permute-done.refs_1_
  12.7 0.1 collective-permute-start.3
  12.7 1.6 %collective-permute-start.6 = (bf16[8,64,128]{2,1,0:T(8,128)(2,1)S(1)}, bf16[8,64,128]{2,1,0:T(8,128)(2,1)S(1)}, u32[]{:S(2)}, u32[]{:S(2)}) collective-permute-start(bf16[8,64,128]{2,1,0:T(8,128)(2,1)S(1)} %collective-permute-done.2.refs_3_), channel_id=1, source_target_pairs={{0,2},{1,3},{2,0},{3,1},{4,6},{5,7},{6,4},{7,5},{8,10},{9,11},{10,... | collective-permute-start | bytes 393224 | tf_op jit(solution)/shard_map/ppermute | solution.py:199
  14.3 1.7 %collective-permute-start.5 = (bf16[8,64,128]{2,1,0:T(8,128)(2,1)S(1)}, bf16[8,64,128]{2,1,0:T(8,128)(2,1)S(1)}, u32[]{:S(2)}, u32[]{:S(2)}) collective-permute-start(bf16[8,64,128]{2,1,0:T(8,128)(2,1)S(1)} %collective-permute-done.2.refs_3_), channel_id=1, source_target_pairs={{0,4},{1,5},{2,6},{3,7},{4,0},{5,1},{6,2},{7,3},{8,12},{9,13},{10,... | collective-permute-start | bytes 393224 | tf_op jit(solution)/shard_map/ppermute | solution.py:199
  16.0 0.6 %collective-permute-start.4 = (bf16[8,64,128]{2,1,0:T(8,128)(2,1)S(1)}, bf16[8,64,128]{2,1,0:T(8,128)(2,1)S(1)}, u32[]{:S(2)}, u32[]{:S(2)}) collective-permute-start(bf16[8,64,128]{2,1,0:T(8,128)(2,1)S(1)} %collective-permute-done.refs_1_), channel_id=1, source_target_pairs={{0,8},{1,9},{2,10},{3,11},{4,12},{5,13},{6,14},{7,15},{8,0},{9,1},... | collective-permute-start | bytes 393224 | tf_op jit(solution)/shard_map/ppermute | solution.py:199
  16.6 2.0 %collective-permute-done.6.refs_2_ = bf16[8,64,128]{2,1,0:T(8,128)(2,1)S(1)} collective-permute-done((bf16[8,64,128]{2,1,0:T(8,128)(2,1)S(1)}, bf16[8,64,128]{2,1,0:T(8,128)(2,1)S(1)}, u32[]{:S(2)}, u32[]{:S(2)}) %collective-permute-start.6) | collective-permute-done | bytes 131104 | tf_op jit(solution)/shard_map/ppermute | solution.py:199
  18.6 1.7 %collective-permute-done.5.refs_1_ = bf16[8,64,128]{2,1,0:T(8,128)(2,1)S(1)} collective-permute-done((bf16[8,64,128]{2,1,0:T(8,128)(2,1)S(1)}, bf16[8,64,128]{2,1,0:T(8,128)(2,1)S(1)}, u32[]{:S(2)}, u32[]{:S(2)}) %collective-permute-start.5) | collective-permute-done | bytes 131104 | tf_op jit(solution)/shard_map/ppermute | solution.py:199
  20.4 4.5 %collective-permute-done.4.refs_0_ = bf16[8,64,128]{2,1,0:T(8,128)(2,1)S(1)} collective-permute-done((bf16[8,64,128]{2,1,0:T(8,128)(2,1)S(1)}, bf16[8,64,128]{2,1,0:T(8,128)(2,1)S(1)}, u32[]{:S(2)}, u32[]{:S(2)}) %collective-permute-start.4) | collective-permute-done | bytes 131104 | tf_op jit(solution)/shard_map/ppermute | solution.py:199
  24.9 0.1 collective-permute-start.7
  25.0 0.6 %collective-permute-start.8 = (bf16[8,64,128]{2,1,0:T(8,128)(2,1)S(1)}, bf16[8,64,128]{2,1,0:T(8,128)(2,1)S(1)}, u32[]{:S(2)}, u32[]{:S(2)}) collective-permute-start(bf16[8,64,128]{2,1,0:T(8,128)(2,1)S(1)} %collective-permute-done.1.refs_2_), channel_id=1, source_target_pairs={{0,2},{1,3},{2,0},{3,1},{4,6},{5,7},{6,4},{7,5},{8,10},{9,11},{10,... | collective-permute-start | bytes 393224 | tf_op jit(solution)/shard_map/ppermute | solution.py:199
  25.6 5.3 %collective-permute-done.8.refs_0_ = bf16[8,64,128]{2,1,0:T(8,128)(2,1)S(1)} collective-permute-done((bf16[8,64,128]{2,1,0:T(8,128)(2,1)S(1)}, bf16[8,64,128]{2,1,0:T(8,128)(2,1)S(1)}, u32[]{:S(2)}, u32[]{:S(2)}) %collective-permute-start.8) | collective-permute-done | bytes 131104 | tf_op jit(solution)/shard_map/ppermute | solution.py:199
  30.9 0.1 collective-permute-start.9
  31.0 2.1 %shard_map.75.x_ref = bf16[112,64,64]{2,1,0:T(8,128)(2,1)S(1)} custom-call(bf16[16,64,64]{2,1,0:T(8,128)(2,1)S(1)} %get-tuple-element.12.p_ref, bf16[16,7,64,64]{3,2,1,0:T(8,128)(2,1)} %a_ref.1), custom_call_target="tpu_custom_call" | custom-call | tf_op jit(solution)/shard_map/pallas_call | solution.py:222
  33.1 1.5 %shard_map.73.code_ref = s32[8,16]{1,0:T(8,128)S(4)} custom-call(s32[7,16]{1,0:T(8,128)} %bitcast.8, s32[7,16]{1,0:T(8,128)} %bitcast.9, s32[1,16]{1,0:T(1,128)} %bitcast.11, s32[7,16]{1,0:T(8,128)} %bitcast.10, s32[1,16]{1,0:T(1,128)} %bitcast.12), custom_call_target="tpu_custom_call" | custom-call | tf_op jit(solution)/shard_map/pallas_call | solution.py:229
  34.6 0.0 collective-permute-done.3.refs_1_
  34.6 0.3 shard_map.77
  34.9 0.0 collective-permute-done.9.refs_3_
  34.9 0.0 collective-permute-done.7.refs_1_
  34.9 0.8 %shard_map.80 = (bf16[1,14,64,128]{3,2,1,0:T(8,128)(2,1)S(1)}, f32[112,64,128]{2,1,0:T(8,128)S(1)}, bf16[128,64,128]{2,1,0:T(8,128)(2,1)S(1)}) custom-call(s32[8,16]{1,0:T(8,128)S(4)} %shard_map.73.code_ref, bf16[112,64,64]{2,1,0:T(8,128)(2,1)S(1)} %shard_map.75.x_ref, ...), custom_call_target="tpu_custom_call", output_to_operand_aliasing={{1}: (2, {}), {2}: (3, {})} | custom-call | tf_op jit(solution)/shard_map/pallas_call | solution.py:246
  35.7 1.6 %collective-permute-start.10 = (bf16[14,64,128]{2,1,0:T(8,128)(2,1)S(1)}, bf16[14,64,128]{2,1,0:T(8,128)(2,1)S(1)}, u32[]{:S(2)}, u32[]{:S(2)}) collective-permute-start(bf16[14,64,128]{2,1,0:T(8,128)(2,1)S(1)} %bitcast.7), channel_id=1, source_target_pairs={{0,16},{16,0},{1,17},{17,1},{2,18},{18,2},{3,19},{19,3},{4,20},{20... | collective-permute-start | bytes 688136 | tf_op jit(solution)/shard_map/ppermute | solution.py:257
  37.3 0.7 %shard_map.81.own_ref = f32[14,64,128]{2,1,0:T(8,128)S(1)} custom-call(s32[8,16]{1,0:T(8,128)S(4)} %shard_map.73.code_ref, bf16[112,64,64]{2,1,0:T(8,128)(2,1)S(1)} %shard_map.75.x_ref, bf16[128,64,128]{2,1,0:T(8,128)(2,1)S(1)} %get-tuple-element.16.gathered_ref, f32[112,64,128]{2,1,0:T(8,128)S(1)} %get-tuple-element.17.acc_in_ref), custom_call_target="tpu_custom_call" | custom-call | tf_op jit(solution)/shard_map/pallas_call | solution.py:260
  38.0 5.8 %collective-permute-done.10.refs_0_ = bf16[14,64,128]{2,1,0:T(8,128)(2,1)S(1)} collective-permute-done((bf16[14,64,128]{2,1,0:T(8,128)(2,1)S(1)}, bf16[14,64,128]{2,1,0:T(8,128)(2,1)S(1)}, u32[]{:S(2)}, u32[]{:S(2)}) %collective-permute-start.10) | collective-permute-done | bytes 229408 | tf_op jit(solution)/shard_map/ppermute | solution.py:257
  43.8 0.9 %shard_map.82 = bf16[28,64,64]{2,1,0:T(8,128)(2,1)} custom-call(f32[14,64,128]{2,1,0:T(8,128)S(1)} %shard_map.81.own_ref, bf16[14,64,128]{2,1,0:T(8,128)(2,1)S(1)} %collective-permute-done.10.refs_0_), custom_call_target="tpu_custom_call" | custom-call | tf_op jit(solution)/shard_map/pallas_call | solution.py:266
  (3 shorter events, 0.1 us)
Async XLA Ops:
  0.0 0.9 %copy-start = (bf16[16,64,64]{2,1,0:T(8,128)(2,1)S(1)}, bf16[16,64,64]{2,1,0:T(8,128)(2,1)}, u32[]{:S(2)}) copy-start(bf16[16,64,64]{2,1,0:T(8,128)(2,1)} %p_ref.1) | copy-start | bytes 393220
  1.1 9.5 %collective-permute-start.2 = (bf16[8,64,128]{2,1,0:T(8,128)(2,1)S(1)}, bf16[8,64,128]{2,1,0:T(8,128)(2,1)S(1)}, u32[]{:S(2)}, u32[]{:S(2)}) collective-permute-start(bf16[8,64,128]{2,1,0:T(8,128)(2,1)S(1)} %get-tuple-element.13.refs_0_), channel_id=1, source_target_pairs={{0,12},{1,13},{2,14},{3,15},{4,8},{5,9},{6,10},{7,11},{8,4},{9,5},... | collective-permute-start | bytes 393224 | tf_op jit(solution)/shard_map/ppermute | solution.py:199
  6.2 6.4 %collective-permute-start.1 = (bf16[8,64,128]{2,1,0:T(8,128)(2,1)S(1)}, bf16[8,64,128]{2,1,0:T(8,128)(2,1)S(1)}, u32[]{:S(2)}, u32[]{:S(2)}) collective-permute-start(bf16[8,64,128]{2,1,0:T(8,128)(2,1)S(1)} %get-tuple-element.13.refs_0_), channel_id=1, source_target_pairs={{0,4},{1,5},{2,6},{3,7},{4,0},{5,1},{6,2},{7,3},{8,12},{9,13},{10,... | collective-permute-start | bytes 393224 | tf_op jit(solution)/shard_map/ppermute | solution.py:199
  6.2 6.4 %collective-permute-start = (bf16[8,64,128]{2,1,0:T(8,128)(2,1)S(1)}, bf16[8,64,128]{2,1,0:T(8,128)(2,1)S(1)}, u32[]{:S(2)}, u32[]{:S(2)}) collective-permute-start(bf16[8,64,128]{2,1,0:T(8,128)(2,1)S(1)} %get-tuple-element.13.refs_0_), channel_id=1, source_target_pairs={{0,2},{1,3},{2,0},{3,1},{4,6},{5,7},{6,4},{7,5},{8,10},{9,11},{10,... | collective-permute-start | bytes 393224 | tf_op jit(solution)/shard_map/ppermute | solution.py:199
  12.7 21.9 %collective-permute-start.3 = (bf16[32,64,128]{2,1,0:T(8,128)(2,1)S(1)}, bf16[32,64,128]{2,1,0:T(8,128)(2,1)S(1)}, u32[]{:S(2)}, u32[]{:S(2)}) collective-permute-start(bf16[32,64,128]{2,1,0:T(8,128)(2,1)S(1)} %shard_map.76.refs_0_), channel_id=1, source_target_pairs={{0,1},{1,0},{2,3},{3,2},{4,5},{5,4},{6,7},{7,6},{8,9},{9,8},{10,11... | collective-permute-start | bytes 1572872 | tf_op jit(solution)/shard_map/ppermute | solution.py:199
  12.7 5.9 %collective-permute-start.6 = (bf16[8,64,128]{2,1,0:T(8,128)(2,1)S(1)}, bf16[8,64,128]{2,1,0:T(8,128)(2,1)S(1)}, u32[]{:S(2)}, u32[]{:S(2)}) collective-permute-start(bf16[8,64,128]{2,1,0:T(8,128)(2,1)S(1)} %collective-permute-done.2.refs_3_), channel_id=1, source_target_pairs={{0,2},{1,3},{2,0},{3,1},{4,6},{5,7},{6,4},{7,5},{8,10},{9,11},{10,... | collective-permute-start | bytes 393224 | tf_op jit(solution)/shard_map/ppermute | solution.py:199
  14.3 6.0 %collective-permute-start.5 = (bf16[8,64,128]{2,1,0:T(8,128)(2,1)S(1)}, bf16[8,64,128]{2,1,0:T(8,128)(2,1)S(1)}, u32[]{:S(2)}, u32[]{:S(2)}) collective-permute-start(bf16[8,64,128]{2,1,0:T(8,128)(2,1)S(1)} %collective-permute-done.2.refs_3_), channel_id=1, source_target_pairs={{0,4},{1,5},{2,6},{3,7},{4,0},{5,1},{6,2},{7,3},{8,12},{9,13},{10,... | collective-permute-start | bytes 393224 | tf_op jit(solution)/shard_map/ppermute | solution.py:199
  16.0 8.9 %collective-permute-start.4 = (bf16[8,64,128]{2,1,0:T(8,128)(2,1)S(1)}, bf16[8,64,128]{2,1,0:T(8,128)(2,1)S(1)}, u32[]{:S(2)}, u32[]{:S(2)}) collective-permute-start(bf16[8,64,128]{2,1,0:T(8,128)(2,1)S(1)} %collective-permute-done.refs_1_), channel_id=1, source_target_pairs={{0,8},{1,9},{2,10},{3,11},{4,12},{5,13},{6,14},{7,15},{8,0},{9,1},... | collective-permute-start | bytes 393224 | tf_op jit(solution)/shard_map/ppermute | solution.py:199
  24.9 10.0 %collective-permute-start.7 = (bf16[24,64,128]{2,1,0:T(8,128)(2,1)S(1)}, bf16[24,64,128]{2,1,0:T(8,128)(2,1)S(1)}, u32[]{:S(2)}, u32[]{:S(2)}) collective-permute-start(bf16[24,64,128]{2,1,0:T(8,128)(2,1)S(1)} %shard_map.78.refs_0_), channel_id=1, source_target_pairs={{0,1},{1,0},{2,3},{3,2},{4,5},{5,4},{6,7},{7,6},{8,9},{9,8},{10,11... | collective-permute-start | bytes 1179656 | tf_op jit(solution)/shard_map/ppermute | solution.py:199
  25.0 5.9 %collective-permute-start.8 = (bf16[8,64,128]{2,1,0:T(8,128)(2,1)S(1)}, bf16[8,64,128]{2,1,0:T(8,128)(2,1)S(1)}, u32[]{:S(2)}, u32[]{:S(2)}) collective-permute-start(bf16[8,64,128]{2,1,0:T(8,128)(2,1)S(1)} %collective-permute-done.1.refs_2_), channel_id=1, source_target_pairs={{0,2},{1,3},{2,0},{3,1},{4,6},{5,7},{6,4},{7,5},{8,10},{9,11},{10,... | collective-permute-start | bytes 393224 | tf_op jit(solution)/shard_map/ppermute | solution.py:199
  30.9 4.0 %collective-permute-start.9 = (bf16[8,64,128]{2,1,0:T(8,128)(2,1)S(1)}, bf16[8,64,128]{2,1,0:T(8,128)(2,1)S(1)}, u32[]{:S(2)}, u32[]{:S(2)}) collective-permute-start(bf16[8,64,128]{2,1,0:T(8,128)(2,1)S(1)} %shard_map.79.refs_2_), channel_id=1, source_target_pairs={{0,1},{1,0},{2,3},{3,2},{4,5},{5,4},{6,7},{7,6},{8,9},{9,8},{10,11... | collective-permute-start | bytes 393224 | tf_op jit(solution)/shard_map/ppermute | solution.py:199
  35.7 8.1 %collective-permute-start.10 = (bf16[14,64,128]{2,1,0:T(8,128)(2,1)S(1)}, bf16[14,64,128]{2,1,0:T(8,128)(2,1)S(1)}, u32[]{:S(2)}, u32[]{:S(2)}) collective-permute-start(bf16[14,64,128]{2,1,0:T(8,128)(2,1)S(1)} %bitcast.7), channel_id=1, source_target_pairs={{0,16},{16,0},{1,17},{17,1},{2,18},{18,2},{3,19},{19,3},{4,20},{20... | collective-permute-start | bytes 688136 | tf_op jit(solution)/shard_map/ppermute | solution.py:257

commit v4 on v3

--- a/solution.py
+++ b/solution.py
@@ -213,10 +213,13 @@
         held[key] = exchange(held[parents[key]], key ^ parents[key])
     pieces = []
     for group in groups:
-        mine = call(
-            merge_kernel, pltpu.VMEM((len(group) * pairs, order, 2 * order), own.dtype),
-            [VMEM] * len(group), VMEM,
-        )(*keep(*[held[key] for key in group]))
+        mine = held[group[0]]
+        if len(group) > 1:
+            mine = call(
+                merge_kernel,
+                pltpu.VMEM((len(group) * pairs, order, 2 * order), own.dtype),
+                [VMEM] * len(group), VMEM,
+            )(*keep(*[held[key] for key in group]))
         pieces += [mine, exchange(mine, 1)]
 
     x = call(

time: 44.9 us -> 44.8 us (level)
  no operation moved by 1% of the time
where the time goes in v4:
time: 44.8 us; the launch traced here: 44.6 us
  waiting for transfers between devices  24.2 us (54%)
  starting transfers between devices  12.9 us (29%)
  Pallas kernels  6.47 us (14%)
  local copies, waits for them, and re-layouts  0.95 us (2%)
    ppermute x10, waiting for transfers between devices, exchange(): return lax.ppermute(array, 'col', [(i, i ^ bits) for i in range(columns)])  18.5 us
    ppermute x10, starting transfers between devices, exchange(): return lax.ppermute(array, 'col', [(i, i ^ bits) for i in range(columns)])  11.3 us
    ppermute x1, waiting for transfers between devices, local(): lax.ppermute(sent[n - 1], 'row', [(i, (i + n) % regions) for i in range(r...  5.79 us
    pallas_call x1, Pallas kernels, local(): call(left_kernel, pltpu.VMEM((rows * entries, order, order), jnp.bfloat16...  2.1 us
    ppermute x1, starting transfers between devices, local(): lax.ppermute(sent[n - 1], 'row', [(i, (i + n) % regions) for i in range(r...  1.56 us
    pallas_call x1, Pallas kernels, local(): call(code_kernel, pltpu.SMEM((entries + 1, rows), jnp.int32), [HBM] * 5,...  1.49 us
    unnamed x2, local copies, waits for them, and re-layouts  0.95 us
    pallas_call x1, Pallas kernels, local(): call(add_kernel, jax.ShapeDtypeStruct((lanes, order, order), jnp.bfloat16...  0.9 us
  transfers between devices with their start and end apart: 11, of which 7 were waited for; matrix products, arithmetic and copies ran while one was open for 0% of the time, Pallas kernels for 10%

profile of v4, /device:TPU:0, one launch (start us, length us, event | category | flops | bytes accessed | tf_op | source)
XLA Modules:
  0.0 44.6 jit_solution(15851057999198584452)
XLA Ops:
  0.0 0.0 copy-start
  0.0 0.9 %copy-done = bf16[16,64,64]{2,1,0:T(8,128)(2,1)S(1)} copy-done((bf16[16,64,64]{2,1,0:T(8,128)(2,1)S(1)}, bf16[16,64,64]{2,1,0:T(8,128)(2,1)}, u32[]{:S(2)}) %copy-start) | copy-done | bytes 131096
  1.0 0.1 shard_map.74
  1.1 5.1 %collective-permute-start.2 = (bf16[8,64,128]{2,1,0:T(8,128)(2,1)S(1)}, bf16[8,64,128]{2,1,0:T(8,128)(2,1)S(1)}, u32[]{:S(2)}, u32[]{:S(2)}) collective-permute-start(bf16[8,64,128]{2,1,0:T(8,128)(2,1)S(1)} %get-tuple-element.13.refs_0_), channel_id=1, source_target_pairs={{0,12},{1,13},{2,14},{3,15},{4,8},{5,9},{6,10},{7,11},{8,4},{9,5},... | collective-permute-start | bytes 393224 | tf_op jit(solution)/shard_map/ppermute | solution.py:199
  6.2 0.0 collective-permute-start.1
  6.2 1.5 %collective-permute-start = (bf16[8,64,128]{2,1,0:T(8,128)(2,1)S(1)}, bf16[8,64,128]{2,1,0:T(8,128)(2,1)S(1)}, u32[]{:S(2)}, u32[]{:S(2)}) collective-permute-start(bf16[8,64,128]{2,1,0:T(8,128)(2,1)S(1)} %get-tuple-element.13.refs_0_), channel_id=1, source_target_pairs={{0,2},{1,3},{2,0},{3,1},{4,6},{5,7},{6,4},{7,5},{8,10},{9,11},{10,... | collective-permute-start | bytes 393224 | tf_op jit(solution)/shard_map/ppermute | solution.py:199
  7.7 2.9 %collective-permute-done.2.refs_3_ = bf16[8,64,128]{2,1,0:T(8,128)(2,1)S(1)} collective-permute-done((bf16[8,64,128]{2,1,0:T(8,128)(2,1)S(1)}, bf16[8,64,128]{2,1,0:T(8,128)(2,1)S(1)}, u32[]{:S(2)}, u32[]{:S(2)}) %collective-permute-start.2) | collective-permute-done | bytes 131104 | tf_op jit(solution)/shard_map/ppermute | solution.py:199
  10.6 2.0 %collective-permute-done.1.refs_2_ = bf16[8,64,128]{2,1,0:T(8,128)(2,1)S(1)} collective-permute-done((bf16[8,64,128]{2,1,0:T(8,128)(2,1)S(1)}, bf16[8,64,128]{2,1,0:T(8,128)(2,1)S(1)}, u32[]{:S(2)}, u32[]{:S(2)}) %collective-permute-start.1) | collective-permute-done | bytes 131104 | tf_op jit(solution)/shard_map/ppermute | solution.py:199
  12.6 0.0 collective-permute-done.refs_1_
  12.7 0.1 collective-permute-start.3
  12.7 1.6 %collective-permute-start.6 = (bf16[8,64,128]{2,1,0:T(8,128)(2,1)S(1)}, bf16[8,64,128]{2,1,0:T(8,128)(2,1)S(1)}, u32[]{:S(2)}, u32[]{:S(2)}) collective-permute-start(bf16[8,64,128]{2,1,0:T(8,128)(2,1)S(1)} %collective-permute-done.2.refs_3_), channel_id=1, source_target_pairs={{0,2},{1,3},{2,0},{3,1},{4,6},{5,7},{6,4},{7,5},{8,10},{9,11},{10,... | collective-permute-start | bytes 393224 | tf_op jit(solution)/shard_map/ppermute | solution.py:199
  14.3 1.7 %collective-permute-start.5 = (bf16[8,64,128]{2,1,0:T(8,128)(2,1)S(1)}, bf16[8,64,128]{2,1,0:T(8,128)(2,1)S(1)}, u32[]{:S(2)}, u32[]{:S(2)}) collective-permute-start(bf16[8,64,128]{2,1,0:T(8,128)(2,1)S(1)} %collective-permute-done.2.refs_3_), channel_id=1, source_target_pairs={{0,4},{1,5},{2,6},{3,7},{4,0},{5,1},{6,2},{7,3},{8,12},{9,13},{10,... | collective-permute-start | bytes 393224 | tf_op jit(solution)/shard_map/ppermute | solution.py:199
  16.0 0.6 %collective-permute-start.4 = (bf16[8,64,128]{2,1,0:T(8,128)(2,1)S(1)}, bf16[8,64,128]{2,1,0:T(8,128)(2,1)S(1)}, u32[]{:S(2)}, u32[]{:S(2)}) collective-permute-start(bf16[8,64,128]{2,1,0:T(8,128)(2,1)S(1)} %collective-permute-done.refs_1_), channel_id=1, source_target_pairs={{0,8},{1,9},{2,10},{3,11},{4,12},{5,13},{6,14},{7,15},{8,0},{9,1},... | collective-permute-start | bytes 393224 | tf_op jit(solution)/shard_map/ppermute | solution.py:199
  16.6 2.0 %collective-permute-done.6.refs_2_ = bf16[8,64,128]{2,1,0:T(8,128)(2,1)S(1)} collective-permute-done((bf16[8,64,128]{2,1,0:T(8,128)(2,1)S(1)}, bf16[8,64,128]{2,1,0:T(8,128)(2,1)S(1)}, u32[]{:S(2)}, u32[]{:S(2)}) %collective-permute-start.6) | collective-permute-done | bytes 131104 | tf_op jit(solution)/shard_map/ppermute | solution.py:199
  18.6 1.7 %collective-permute-done.5.refs_1_ = bf16[8,64,128]{2,1,0:T(8,128)(2,1)S(1)} collective-permute-done((bf16[8,64,128]{2,1,0:T(8,128)(2,1)S(1)}, bf16[8,64,128]{2,1,0:T(8,128)(2,1)S(1)}, u32[]{:S(2)}, u32[]{:S(2)}) %collective-permute-start.5) | collective-permute-done | bytes 131104 | tf_op jit(solution)/shard_map/ppermute | solution.py:199
  20.4 4.5 %collective-permute-done.4.refs_0_ = bf16[8,64,128]{2,1,0:T(8,128)(2,1)S(1)} collective-permute-done((bf16[8,64,128]{2,1,0:T(8,128)(2,1)S(1)}, bf16[8,64,128]{2,1,0:T(8,128)(2,1)S(1)}, u32[]{:S(2)}, u32[]{:S(2)}) %collective-permute-start.4) | collective-permute-done | bytes 131104 | tf_op jit(solution)/shard_map/ppermute | solution.py:199
  24.9 0.1 collective-permute-start.7
  25.0 0.6 %collective-permute-start.8 = (bf16[8,64,128]{2,1,0:T(8,128)(2,1)S(1)}, bf16[8,64,128]{2,1,0:T(8,128)(2,1)S(1)}, u32[]{:S(2)}, u32[]{:S(2)}) collective-permute-start(bf16[8,64,128]{2,1,0:T(8,128)(2,1)S(1)} %collective-permute-done.1.refs_2_), channel_id=1, source_target_pairs={{0,2},{1,3},{2,0},{3,1},{4,6},{5,7},{6,4},{7,5},{8,10},{9,11},{10,... | collective-permute-start | bytes 393224 | tf_op jit(solution)/shard_map/ppermute | solution.py:199
  25.6 5.3 %collective-permute-done.8.refs_2_ = bf16[8,64,128]{2,1,0:T(8,128)(2,1)S(1)} collective-permute-done((bf16[8,64,128]{2,1,0:T(8,128)(2,1)S(1)}, bf16[8,64,128]{2,1,0:T(8,128)(2,1)S(1)}, u32[]{:S(2)}, u32[]{:S(2)}) %collective-permute-start.8) | collective-permute-done | bytes 131104 | tf_op jit(solution)/shard_map/ppermute | solution.py:199
  30.9 0.0 collective-permute-start.9
  30.9 2.1 %shard_map.75.x_ref = bf16[112,64,64]{2,1,0:T(8,128)(2,1)S(1)} custom-call(bf16[16,64,64]{2,1,0:T(8,128)(2,1)S(1)} %get-tuple-element.12.p_ref, bf16[16,7,64,64]{3,2,1,0:T(8,128)(2,1)} %a_ref.1), custom_call_target="tpu_custom_call" | custom-call | tf_op jit(solution)/shard_map/pallas_call | solution.py:225
  33.0 1.5 %shard_map.73.code_ref = s32[8,16]{1,0:T(8,128)S(4)} custom-call(s32[7,16]{1,0:T(8,128)} %bitcast.8, s32[7,16]{1,0:T(8,128)} %bitcast.9, s32[1,16]{1,0:T(1,128)} %bitcast.11, s32[7,16]{1,0:T(8,128)} %bitcast.10, s32[1,16]{1,0:T(1,128)} %bitcast.12), custom_call_target="tpu_custom_call" | custom-call | tf_op jit(solution)/shard_map/pallas_call | solution.py:232
  34.5 0.0 collective-permute-done.3.refs_1_
  34.5 0.3 shard_map.77
  34.8 0.0 collective-permute-done.9.refs_3_
  34.8 0.0 collective-permute-done.7.refs_1_
  34.8 0.8 %shard_map.79 = (bf16[1,14,64,128]{3,2,1,0:T(8,128)(2,1)S(1)}, f32[112,64,128]{2,1,0:T(8,128)S(1)}, bf16[128,64,128]{2,1,0:T(8,128)(2,1)S(1)}) custom-call(s32[8,16]{1,0:T(8,128)S(4)} %shard_map.73.code_ref, bf16[112,64,64]{2,1,0:T(8,128)(2,1)S(1)} %shard_map.75.x_ref, ...), custom_call_target="tpu_custom_call", output_to_operand_aliasing={{1}: (2, {}), {2}: (3, {})} | custom-call | tf_op jit(solution)/shard_map/pallas_call | solution.py:249
  35.6 1.6 %collective-permute-start.10 = (bf16[14,64,128]{2,1,0:T(8,128)(2,1)S(1)}, bf16[14,64,128]{2,1,0:T(8,128)(2,1)S(1)}, u32[]{:S(2)}, u32[]{:S(2)}) collective-permute-start(bf16[14,64,128]{2,1,0:T(8,128)(2,1)S(1)} %bitcast.7), channel_id=1, source_target_pairs={{0,16},{16,0},{1,17},{17,1},{2,18},{18,2},{3,19},{19,3},{4,20},{20... | collective-permute-start | bytes 688136 | tf_op jit(solution)/shard_map/ppermute | solution.py:260
  37.2 0.7 %shard_map.80.own_ref = f32[14,64,128]{2,1,0:T(8,128)S(1)} custom-call(s32[8,16]{1,0:T(8,128)S(4)} %shard_map.73.code_ref, bf16[112,64,64]{2,1,0:T(8,128)(2,1)S(1)} %shard_map.75.x_ref, bf16[128,64,128]{2,1,0:T(8,128)(2,1)S(1)} %get-tuple-element.16.gathered_ref, f32[112,64,128]{2,1,0:T(8,128)S(1)} %get-tuple-element.17.acc_in_ref), custom_call_target="tpu_custom_call" | custom-call | tf_op jit(solution)/shard_map/pallas_call | solution.py:263
  37.9 5.8 %collective-permute-done.10.refs_0_ = bf16[14,64,128]{2,1,0:T(8,128)(2,1)S(1)} collective-permute-done((bf16[14,64,128]{2,1,0:T(8,128)(2,1)S(1)}, bf16[14,64,128]{2,1,0:T(8,128)(2,1)S(1)}, u32[]{:S(2)}, u32[]{:S(2)}) %collective-permute-start.10) | collective-permute-done | bytes 229408 | tf_op jit(solution)/shard_map/ppermute | solution.py:260
  43.7 0.9 %shard_map.81 = bf16[28,64,64]{2,1,0:T(8,128)(2,1)} custom-call(f32[14,64,128]{2,1,0:T(8,128)S(1)} %shard_map.80.own_ref, bf16[14,64,128]{2,1,0:T(8,128)(2,1)S(1)} %collective-permute-done.10.refs_0_), custom_call_target="tpu_custom_call" | custom-call | tf_op jit(solution)/shard_map/pallas_call | solution.py:269
  (2 shorter events, 0.1 us)
Async XLA Ops:
  0.0 0.9 %copy-start = (bf16[16,64,64]{2,1,0:T(8,128)(2,1)S(1)}, bf16[16,64,64]{2,1,0:T(8,128)(2,1)}, u32[]{:S(2)}) copy-start(bf16[16,64,64]{2,1,0:T(8,128)(2,1)} %p_ref.1) | copy-start | bytes 393220
  1.1 9.5 %collective-permute-start.2 = (bf16[8,64,128]{2,1,0:T(8,128)(2,1)S(1)}, bf16[8,64,128]{2,1,0:T(8,128)(2,1)S(1)}, u32[]{:S(2)}, u32[]{:S(2)}) collective-permute-start(bf16[8,64,128]{2,1,0:T(8,128)(2,1)S(1)} %get-tuple-element.13.refs_0_), channel_id=1, source_target_pairs={{0,12},{1,13},{2,14},{3,15},{4,8},{5,9},{6,10},{7,11},{8,4},{9,5},... | collective-permute-start | bytes 393224 | tf_op jit(solution)/shard_map/ppermute | solution.py:199
  6.2 6.4 %collective-permute-start.1 = (bf16[8,64,128]{2,1,0:T(8,128)(2,1)S(1)}, bf16[8,64,128]{2,1,0:T(8,128)(2,1)S(1)}, u32[]{:S(2)}, u32[]{:S(2)}) collective-permute-start(bf16[8,64,128]{2,1,0:T(8,128)(2,1)S(1)} %get-tuple-element.13.refs_0_), channel_id=1, source_target_pairs={{0,4},{1,5},{2,6},{3,7},{4,0},{5,1},{6,2},{7,3},{8,12},{9,13},{10,... | collective-permute-start | bytes 393224 | tf_op jit(solution)/shard_map/ppermute | solution.py:199
  6.2 6.4 %collective-permute-start = (bf16[8,64,128]{2,1,0:T(8,128)(2,1)S(1)}, bf16[8,64,128]{2,1,0:T(8,128)(2,1)S(1)}, u32[]{:S(2)}, u32[]{:S(2)}) collective-permute-start(bf16[8,64,128]{2,1,0:T(8,128)(2,1)S(1)} %get-tuple-element.13.refs_0_), channel_id=1, source_target_pairs={{0,2},{1,3},{2,0},{3,1},{4,6},{5,7},{6,4},{7,5},{8,10},{9,11},{10,... | collective-permute-start | bytes 393224 | tf_op jit(solution)/shard_map/ppermute | solution.py:199
  12.7 21.8 %collective-permute-start.3 = (bf16[32,64,128]{2,1,0:T(8,128)(2,1)S(1)}, bf16[32,64,128]{2,1,0:T(8,128)(2,1)S(1)}, u32[]{:S(2)}, u32[]{:S(2)}) collective-permute-start(bf16[32,64,128]{2,1,0:T(8,128)(2,1)S(1)} %shard_map.76.refs_0_), channel_id=1, source_target_pairs={{0,1},{1,0},{2,3},{3,2},{4,5},{5,4},{6,7},{7,6},{8,9},{9,8},{10,11... | collective-permute-start | bytes 1572872 | tf_op jit(solution)/shard_map/ppermute | solution.py:199
  12.7 5.9 %collective-permute-start.6 = (bf16[8,64,128]{2,1,0:T(8,128)(2,1)S(1)}, bf16[8,64,128]{2,1,0:T(8,128)(2,1)S(1)}, u32[]{:S(2)}, u32[]{:S(2)}) collective-permute-start(bf16[8,64,128]{2,1,0:T(8,128)(2,1)S(1)} %collective-permute-done.2.refs_3_), channel_id=1, source_target_pairs={{0,2},{1,3},{2,0},{3,1},{4,6},{5,7},{6,4},{7,5},{8,10},{9,11},{10,... | collective-permute-start | bytes 393224 | tf_op jit(solution)/shard_map/ppermute | solution.py:199
  14.3 6.0 %collective-permute-start.5 = (bf16[8,64,128]{2,1,0:T(8,128)(2,1)S(1)}, bf16[8,64,128]{2,1,0:T(8,128)(2,1)S(1)}, u32[]{:S(2)}, u32[]{:S(2)}) collective-permute-start(bf16[8,64,128]{2,1,0:T(8,128)(2,1)S(1)} %collective-permute-done.2.refs_3_), channel_id=1, source_target_pairs={{0,4},{1,5},{2,6},{3,7},{4,0},{5,1},{6,2},{7,3},{8,12},{9,13},{10,... | collective-permute-start | bytes 393224 | tf_op jit(solution)/shard_map/ppermute | solution.py:199
  16.0 8.9 %collective-permute-start.4 = (bf16[8,64,128]{2,1,0:T(8,128)(2,1)S(1)}, bf16[8,64,128]{2,1,0:T(8,128)(2,1)S(1)}, u32[]{:S(2)}, u32[]{:S(2)}) collective-permute-start(bf16[8,64,128]{2,1,0:T(8,128)(2,1)S(1)} %collective-permute-done.refs_1_), channel_id=1, source_target_pairs={{0,8},{1,9},{2,10},{3,11},{4,12},{5,13},{6,14},{7,15},{8,0},{9,1},... | collective-permute-start | bytes 393224 | tf_op jit(solution)/shard_map/ppermute | solution.py:199
  24.9 9.9 %collective-permute-start.7 = (bf16[24,64,128]{2,1,0:T(8,128)(2,1)S(1)}, bf16[24,64,128]{2,1,0:T(8,128)(2,1)S(1)}, u32[]{:S(2)}, u32[]{:S(2)}) collective-permute-start(bf16[24,64,128]{2,1,0:T(8,128)(2,1)S(1)} %shard_map.78.refs_0_), channel_id=1, source_target_pairs={{0,1},{1,0},{2,3},{3,2},{4,5},{5,4},{6,7},{7,6},{8,9},{9,8},{10,11... | collective-permute-start | bytes 1179656 | tf_op jit(solution)/shard_map/ppermute | solution.py:199
  25.0 5.9 %collective-permute-start.8 = (bf16[8,64,128]{2,1,0:T(8,128)(2,1)S(1)}, bf16[8,64,128]{2,1,0:T(8,128)(2,1)S(1)}, u32[]{:S(2)}, u32[]{:S(2)}) collective-permute-start(bf16[8,64,128]{2,1,0:T(8,128)(2,1)S(1)} %collective-permute-done.1.refs_2_), channel_id=1, source_target_pairs={{0,2},{1,3},{2,0},{3,1},{4,6},{5,7},{6,4},{7,5},{8,10},{9,11},{10,... | collective-permute-start | bytes 393224 | tf_op jit(solution)/shard_map/ppermute | solution.py:199
  30.9 3.9 %collective-permute-start.9 = (bf16[8,64,128]{2,1,0:T(8,128)(2,1)S(1)}, bf16[8,64,128]{2,1,0:T(8,128)(2,1)S(1)}, u32[]{:S(2)}, u32[]{:S(2)}) collective-permute-start(bf16[8,64,128]{2,1,0:T(8,128)(2,1)S(1)} %collective-permute-done.8.refs_2_), channel_id=1, source_target_pairs={{0,1},{1,0},{2,3},{3,2},{4,5},{5,4},{6,7},{7,6},{8,9},{9,8},{10,11... | collective-permute-start | bytes 393224 | tf_op jit(solution)/shard_map/ppermute | solution.py:199
  35.6 8.1 %collective-permute-start.10 = (bf16[14,64,128]{2,1,0:T(8,128)(2,1)S(1)}, bf16[14,64,128]{2,1,0:T(8,128)(2,1)S(1)}, u32[]{:S(2)}, u32[]{:S(2)}) collective-permute-start(bf16[14,64,128]{2,1,0:T(8,128)(2,1)S(1)} %bitcast.7), channel_id=1, source_target_pairs={{0,16},{16,0},{1,17},{17,1},{2,18},{18,2},{3,19},{19,3},{4,20},{20... | collective-permute-start | bytes 688136 | tf_op jit(solution)/shard_map/ppermute | solution.py:260

commit v5 on v4

--- a/solution.py
+++ b/solution.py
@@ -13,7 +13,7 @@
 SMEM = pl.BlockSpec(memory_space=pltpu.SMEM)
 HBM = pl.BlockSpec(memory_space=pltpu.HBM)
 LIMIT = 1 << 20
-PARTS = 2
+PARTS = 1
 
 
 def keep(*arrays):
@@ -140,17 +140,21 @@
     return lax.broadcasted_iota(jnp.int32, (order, width), 1) < width // 2
 
 
-def ready_kernel(*refs):
+def place(starts, pieces, gathered_ref):
+    for start, piece in zip(starts, pieces):
+        gathered_ref[start : start + piece.shape[0]] = piece[...]
+
+
+def ready_kernel(starts, *refs):
     *pieces, acc_ref, gathered_ref = refs
     acc_ref[...] = jnp.zeros_like(acc_ref)
-    merge_kernel(*pieces, gathered_ref)
-
-
-def away_kernel(visits, code_ref, x_ref, acc_in_ref, gathered_in_ref, *refs):
+    place(starts, pieces, gathered_ref)
+
+
+def away_kernel(visits, starts, code_ref, x_ref, acc_in_ref, gathered_in_ref, *refs):
     *pieces, sent_ref, acc_ref, gathered_ref = refs
     regions, half, order, width = sent_ref.shape
-    start = gathered_ref.shape[0] - sum(piece.shape[0] for piece in pieces)
-    merge_kernel(*pieces, gathered_ref.at[start:])
+    place(starts, pieces, gathered_ref)
     accumulate(range(visits), code_ref, x_ref, gathered_ref, acc_ref)
     low = lower_half(order, width)
     for n in range(regions):
@@ -241,20 +245,23 @@
     most = -(-rows // regions) + 1
     visits_away = min(rows, (regions - 1) * most)
     code = pltpu.with_memory_space_constraint(code, pltpu.SMEM)
+    starts = [sum(piece.shape[0] for piece in pieces[:n]) for n in range(len(pieces))]
+    late = [n for n in range(3, len(pieces), 2)]
+    soon = [n for n in range(len(pieces)) if n not in late]
     sums, gathered = call(
-        ready_kernel,
+        functools.partial(ready_kernel, [starts[n] for n in soon]),
         (pltpu.VMEM(acc, jnp.float32), pltpu.VMEM((columns * pairs, order, width), p_blocks.dtype)),
-        [VMEM] * 2, (VMEM, VMEM),
-    )(*keep(*pieces[:2]))
+        [VMEM] * len(soon), (VMEM, VMEM),
+    )(*keep(*[pieces[n] for n in soon]))
     sent, sums, gathered = call(
-        functools.partial(away_kernel, visits_away),
+        functools.partial(away_kernel, visits_away, [starts[n] for n in late]),
         (
             pltpu.VMEM((regions - 1, half, order, width), jnp.bfloat16),
             pltpu.VMEM(acc, jnp.float32),
             pltpu.VMEM((columns * pairs, order, width), p_blocks.dtype),
         ),
-        [SMEM] + [VMEM] * (1 + len(pieces)), (VMEM, VMEM, VMEM), aliases={2: 1, 3: 2},
-    )(code, *keep(x, sums, gathered, *pieces[2:]))
+        [SMEM] + [VMEM] * (3 + len(late)), (VMEM, VMEM, VMEM), aliases={2: 1, 3: 2},
+    )(code, *keep(x, sums, gathered, *[pieces[n] for n in late]))
 
     received = [
         lax.ppermute(sent[n - 1], "row", [(i, (i + n) % regions) for i in range(regions)])

time: 44.8 us -> 44.9 us (level)
  transfers between devices with their start and end apart: 11 -> 11, of which waited for: 7 -> 7; matrix products, arithmetic and copies ran while one was open for 0% -> 0% of each run, Pallas kernels for 10% -> 11%
where the time goes in v5:
time: 44.9 us; the launch traced here: 44.7 us
  waiting for transfers between devices  24.2 us (54%)
  starting transfers between devices  12.9 us (29%)
  Pallas kernels  6.57 us (15%)
  local copies, waits for them, and re-layouts  0.95 us (2%)
    ppermute x10, waiting for transfers between devices, exchange(): return lax.ppermute(array, 'col', [(i, i ^ bits) for i in range(columns)])  18.5 us
    ppermute x10, starting transfers between devices, exchange(): return lax.ppermute(array, 'col', [(i, i ^ bits) for i in range(columns)])  11.3 us
    ppermute x1, waiting for transfers between devices, local(): lax.ppermute(sent[n - 1], 'row', [(i, (i + n) % regions) for i in range(r...  5.78 us
    pallas_call x1, Pallas kernels, local(): call(left_kernel, pltpu.VMEM((rows * entries, order, order), jnp.bfloat16...  2.2 us
    ppermute x1, starting transfers between devices, local(): lax.ppermute(sent[n - 1], 'row', [(i, (i + n) % regions) for i in range(r...  1.56 us
    pallas_call x1, Pallas kernels, local(): call(code_kernel, pltpu.SMEM((entries + 1, rows), jnp.int32), [HBM] * 5,...  1.49 us
    unnamed x2, local copies, waits for them, and re-layouts  0.95 us
    pallas_call x1, Pallas kernels, local(): call(add_kernel, jax.ShapeDtypeStruct((lanes, order, order), jnp.bfloat16...  0.9 us
  transfers between devices with their start and end apart: 11, of which 7 were waited for; matrix products, arithmetic and copies ran while one was open for 0% of the time, Pallas kernels for 11%

profile of v5, /device:TPU:0, one launch (start us, length us, event | category | flops | bytes accessed | tf_op | source)
XLA Modules:
  0.0 44.7 jit_solution(16400537314449761292)
XLA Ops:
  0.0 0.0 copy-start
  0.0 0.9 %copy-done = bf16[16,64,64]{2,1,0:T(8,128)(2,1)S(1)} copy-done((bf16[16,64,64]{2,1,0:T(8,128)(2,1)S(1)}, bf16[16,64,64]{2,1,0:T(8,128)(2,1)}, u32[]{:S(2)}) %copy-start) | copy-done | bytes 131096
  1.0 0.1 shard_map.74
  1.1 5.1 %collective-permute-start.2 = (bf16[8,64,128]{2,1,0:T(8,128)(2,1)S(1)}, bf16[8,64,128]{2,1,0:T(8,128)(2,1)S(1)}, u32[]{:S(2)}, u32[]{:S(2)}) collective-permute-start(bf16[8,64,128]{2,1,0:T(8,128)(2,1)S(1)} %get-tuple-element.13.refs_0_), channel_id=1, source_target_pairs={{0,12},{1,13},{2,14},{3,15},{4,8},{5,9},{6,10},{7,11},{8,4},{9,5},... | collective-permute-start | bytes 393224 | tf_op jit(solution)/shard_map/ppermute | solution.py:203
  6.2 0.0 collective-permute-start.1
  6.2 1.5 %collective-permute-start = (bf16[8,64,128]{2,1,0:T(8,128)(2,1)S(1)}, bf16[8,64,128]{2,1,0:T(8,128)(2,1)S(1)}, u32[]{:S(2)}, u32[]{:S(2)}) collective-permute-start(bf16[8,64,128]{2,1,0:T(8,128)(2,1)S(1)} %get-tuple-element.13.refs_0_), channel_id=1, source_target_pairs={{0,2},{1,3},{2,0},{3,1},{4,6},{5,7},{6,4},{7,5},{8,10},{9,11},{10,... | collective-permute-start | bytes 393224 | tf_op jit(solution)/shard_map/ppermute | solution.py:203
  7.7 2.9 %collective-permute-done.2.refs_3_ = bf16[8,64,128]{2,1,0:T(8,128)(2,1)S(1)} collective-permute-done((bf16[8,64,128]{2,1,0:T(8,128)(2,1)S(1)}, bf16[8,64,128]{2,1,0:T(8,128)(2,1)S(1)}, u32[]{:S(2)}, u32[]{:S(2)}) %collective-permute-start.2) | collective-permute-done | bytes 131104 | tf_op jit(solution)/shard_map/ppermute | solution.py:203
  10.6 2.0 %collective-permute-done.1.refs_2_ = bf16[8,64,128]{2,1,0:T(8,128)(2,1)S(1)} collective-permute-done((bf16[8,64,128]{2,1,0:T(8,128)(2,1)S(1)}, bf16[8,64,128]{2,1,0:T(8,128)(2,1)S(1)}, u32[]{:S(2)}, u32[]{:S(2)}) %collective-permute-start.1) | collective-permute-done | bytes 131104 | tf_op jit(solution)/shard_map/ppermute | solution.py:203
  12.6 0.0 collective-permute-done.refs_1_
  12.7 0.1 collective-permute-start.3
  12.7 1.6 %collective-permute-start.6 = (bf16[8,64,128]{2,1,0:T(8,128)(2,1)S(1)}, bf16[8,64,128]{2,1,0:T(8,128)(2,1)S(1)}, u32[]{:S(2)}, u32[]{:S(2)}) collective-permute-start(bf16[8,64,128]{2,1,0:T(8,128)(2,1)S(1)} %collective-permute-done.2.refs_3_), channel_id=1, source_target_pairs={{0,2},{1,3},{2,0},{3,1},{4,6},{5,7},{6,4},{7,5},{8,10},{9,11},{10,... | collective-permute-start | bytes 393224 | tf_op jit(solution)/shard_map/ppermute | solution.py:203
  14.3 1.7 %collective-permute-start.5 = (bf16[8,64,128]{2,1,0:T(8,128)(2,1)S(1)}, bf16[8,64,128]{2,1,0:T(8,128)(2,1)S(1)}, u32[]{:S(2)}, u32[]{:S(2)}) collective-permute-start(bf16[8,64,128]{2,1,0:T(8,128)(2,1)S(1)} %collective-permute-done.2.refs_3_), channel_id=1, source_target_pairs={{0,4},{1,5},{2,6},{3,7},{4,0},{5,1},{6,2},{7,3},{8,12},{9,13},{10,... | collective-permute-start | bytes 393224 | tf_op jit(solution)/shard_map/ppermute | solution.py:203
  16.0 0.6 %collective-permute-start.4 = (bf16[8,64,128]{2,1,0:T(8,128)(2,1)S(1)}, bf16[8,64,128]{2,1,0:T(8,128)(2,1)S(1)}, u32[]{:S(2)}, u32[]{:S(2)}) collective-permute-start(bf16[8,64,128]{2,1,0:T(8,128)(2,1)S(1)} %collective-permute-done.refs_1_), channel_id=1, source_target_pairs={{0,8},{1,9},{2,10},{3,11},{4,12},{5,13},{6,14},{7,15},{8,0},{9,1},... | collective-permute-start | bytes 393224 | tf_op jit(solution)/shard_map/ppermute | solution.py:203
  16.6 2.0 %collective-permute-done.6.refs_2_ = bf16[8,64,128]{2,1,0:T(8,128)(2,1)S(1)} collective-permute-done((bf16[8,64,128]{2,1,0:T(8,128)(2,1)S(1)}, bf16[8,64,128]{2,1,0:T(8,128)(2,1)S(1)}, u32[]{:S(2)}, u32[]{:S(2)}) %collective-permute-start.6) | collective-permute-done | bytes 131104 | tf_op jit(solution)/shard_map/ppermute | solution.py:203
  18.6 1.7 %collective-permute-done.5.refs_1_ = bf16[8,64,128]{2,1,0:T(8,128)(2,1)S(1)} collective-permute-done((bf16[8,64,128]{2,1,0:T(8,128)(2,1)S(1)}, bf16[8,64,128]{2,1,0:T(8,128)(2,1)S(1)}, u32[]{:S(2)}, u32[]{:S(2)}) %collective-permute-start.5) | collective-permute-done | bytes 131104 | tf_op jit(solution)/shard_map/ppermute | solution.py:203
  20.4 4.5 %collective-permute-done.4.refs_0_ = bf16[8,64,128]{2,1,0:T(8,128)(2,1)S(1)} collective-permute-done((bf16[8,64,128]{2,1,0:T(8,128)(2,1)S(1)}, bf16[8,64,128]{2,1,0:T(8,128)(2,1)S(1)}, u32[]{:S(2)}, u32[]{:S(2)}) %collective-permute-start.4) | collective-permute-done | bytes 131104 | tf_op jit(solution)/shard_map/ppermute | solution.py:203
  24.9 0.1 collective-permute-start.8
  25.0 0.6 %collective-permute-start.7 = (bf16[8,64,128]{2,1,0:T(8,128)(2,1)S(1)}, bf16[8,64,128]{2,1,0:T(8,128)(2,1)S(1)}, u32[]{:S(2)}, u32[]{:S(2)}) collective-permute-start(bf16[8,64,128]{2,1,0:T(8,128)(2,1)S(1)} %collective-permute-done.1.refs_2_), channel_id=1, source_target_pairs={{0,2},{1,3},{2,0},{3,1},{4,6},{5,7},{6,4},{7,5},{8,10},{9,11},{10,... | collective-permute-start | bytes 393224 | tf_op jit(solution)/shard_map/ppermute | solution.py:203
  25.6 5.3 %collective-permute-done.7.refs_3_ = bf16[8,64,128]{2,1,0:T(8,128)(2,1)S(1)} collective-permute-done((bf16[8,64,128]{2,1,0:T(8,128)(2,1)S(1)}, bf16[8,64,128]{2,1,0:T(8,128)(2,1)S(1)}, u32[]{:S(2)}, u32[]{:S(2)}) %collective-permute-start.7) | collective-permute-done | bytes 131104 | tf_op jit(solution)/shard_map/ppermute | solution.py:203
  30.9 0.0 collective-permute-start.9
  30.9 2.2 %shard_map.75.x_ref = bf16[112,64,64]{2,1,0:T(8,128)(2,1)S(1)} custom-call(bf16[16,64,64]{2,1,0:T(8,128)(2,1)S(1)} %get-tuple-element.12.p_ref, bf16[16,7,64,64]{3,2,1,0:T(8,128)(2,1)} %a_ref.1), custom_call_target="tpu_custom_call" | custom-call | tf_op jit(solution)/shard_map/pallas_call | solution.py:229
  33.1 1.5 %shard_map.73.code_ref = s32[8,16]{1,0:T(8,128)S(4)} custom-call(s32[7,16]{1,0:T(8,128)} %bitcast.8, s32[7,16]{1,0:T(8,128)} %bitcast.9, s32[1,16]{1,0:T(1,128)} %bitcast.11, s32[7,16]{1,0:T(8,128)} %bitcast.10, s32[1,16]{1,0:T(1,128)} %bitcast.12), custom_call_target="tpu_custom_call" | custom-call | tf_op jit(solution)/shard_map/pallas_call | solution.py:236
  34.6 0.0 collective-permute-done.3.refs_1_
  34.6 0.3 shard_map.78
  34.9 0.0 collective-permute-done.9.refs_1_
  35.0 0.0 collective-permute-done.8.refs_0_
  35.0 0.8 %shard_map.79 = (bf16[1,14,64,128]{3,2,1,0:T(8,128)(2,1)S(1)}, f32[112,64,128]{2,1,0:T(8,128)S(1)}, bf16[128,64,128]{2,1,0:T(8,128)(2,1)S(1)}) custom-call(s32[8,16]{1,0:T(8,128)S(4)} %shard_map.73.code_ref, bf16[112,64,64]{2,1,0:T(8,128)(2,1)S(1)} %shard_map.75.x_ref, ...), custom_call_target="tpu_custom_call", output_to_operand_aliasing={{1}: (2, {}), {2}: (3, {})} | custom-call | tf_op jit(solution)/shard_map/pallas_call | solution.py:256
  35.7 1.6 %collective-permute-start.10 = (bf16[14,64,128]{2,1,0:T(8,128)(2,1)S(1)}, bf16[14,64,128]{2,1,0:T(8,128)(2,1)S(1)}, u32[]{:S(2)}, u32[]{:S(2)}) collective-permute-start(bf16[14,64,128]{2,1,0:T(8,128)(2,1)S(1)} %bitcast.7), channel_id=1, source_target_pairs={{0,16},{16,0},{1,17},{17,1},{2,18},{18,2},{3,19},{19,3},{4,20},{20... | collective-permute-start | bytes 688136 | tf_op jit(solution)/shard_map/ppermute | solution.py:267
  37.3 0.7 %shard_map.80.own_ref = f32[14,64,128]{2,1,0:T(8,128)S(1)} custom-call(s32[8,16]{1,0:T(8,128)S(4)} %shard_map.73.code_ref, bf16[112,64,64]{2,1,0:T(8,128)(2,1)S(1)} %shard_map.75.x_ref, bf16[128,64,128]{2,1,0:T(8,128)(2,1)S(1)} %get-tuple-element.16.gathered_ref, f32[112,64,128]{2,1,0:T(8,128)S(1)} %get-tuple-element.17.acc_in_ref), custom_call_target="tpu_custom_call" | custom-call | tf_op jit(solution)/shard_map/pallas_call | solution.py:270
  38.0 5.8 %collective-permute-done.10.refs_0_ = bf16[14,64,128]{2,1,0:T(8,128)(2,1)S(1)} collective-permute-done((bf16[14,64,128]{2,1,0:T(8,128)(2,1)S(1)}, bf16[14,64,128]{2,1,0:T(8,128)(2,1)S(1)}, u32[]{:S(2)}, u32[]{:S(2)}) %collective-permute-start.10) | collective-permute-done | bytes 229408 | tf_op jit(solution)/shard_map/ppermute | solution.py:267
  43.8 0.9 %shard_map.81 = bf16[28,64,64]{2,1,0:T(8,128)(2,1)} custom-call(f32[14,64,128]{2,1,0:T(8,128)S(1)} %shard_map.80.own_ref, bf16[14,64,128]{2,1,0:T(8,128)(2,1)S(1)} %collective-permute-done.10.refs_0_), custom_call_target="tpu_custom_call" | custom-call | tf_op jit(solution)/shard_map/pallas_call | solution.py:276
  (2 shorter events, 0.1 us)
Async XLA Ops:
  0.0 0.9 %copy-start = (bf16[16,64,64]{2,1,0:T(8,128)(2,1)S(1)}, bf16[16,64,64]{2,1,0:T(8,128)(2,1)}, u32[]{:S(2)}) copy-start(bf16[16,64,64]{2,1,0:T(8,128)(2,1)} %p_ref.1) | copy-start | bytes 393220
  1.1 9.5 %collective-permute-start.2 = (bf16[8,64,128]{2,1,0:T(8,128)(2,1)S(1)}, bf16[8,64,128]{2,1,0:T(8,128)(2,1)S(1)}, u32[]{:S(2)}, u32[]{:S(2)}) collective-permute-start(bf16[8,64,128]{2,1,0:T(8,128)(2,1)S(1)} %get-tuple-element.13.refs_0_), channel_id=1, source_target_pairs={{0,12},{1,13},{2,14},{3,15},{4,8},{5,9},{6,10},{7,11},{8,4},{9,5},... | collective-permute-start | bytes 393224 | tf_op jit(solution)/shard_map/ppermute | solution.py:203
  6.2 6.4 %collective-permute-start.1 = (bf16[8,64,128]{2,1,0:T(8,128)(2,1)S(1)}, bf16[8,64,128]{2,1,0:T(8,128)(2,1)S(1)}, u32[]{:S(2)}, u32[]{:S(2)}) collective-permute-start(bf16[8,64,128]{2,1,0:T(8,128)(2,1)S(1)} %get-tuple-element.13.refs_0_), channel_id=1, source_target_pairs={{0,4},{1,5},{2,6},{3,7},{4,0},{5,1},{6,2},{7,3},{8,12},{9,13},{10,... | collective-permute-start | bytes 393224 | tf_op jit(solution)/shard_map/ppermute | solution.py:203
  6.2 6.4 %collective-permute-start = (bf16[8,64,128]{2,1,0:T(8,128)(2,1)S(1)}, bf16[8,64,128]{2,1,0:T(8,128)(2,1)S(1)}, u32[]{:S(2)}, u32[]{:S(2)}) collective-permute-start(bf16[8,64,128]{2,1,0:T(8,128)(2,1)S(1)} %get-tuple-element.13.refs_0_), channel_id=1, source_target_pairs={{0,2},{1,3},{2,0},{3,1},{4,6},{5,7},{6,4},{7,5},{8,10},{9,11},{10,... | collective-permute-start | bytes 393224 | tf_op jit(solution)/shard_map/ppermute | solution.py:203
  12.7 21.9 %collective-permute-start.3 = (bf16[32,64,128]{2,1,0:T(8,128)(2,1)S(1)}, bf16[32,64,128]{2,1,0:T(8,128)(2,1)S(1)}, u32[]{:S(2)}, u32[]{:S(2)}) collective-permute-start(bf16[32,64,128]{2,1,0:T(8,128)(2,1)S(1)} %shard_map.76.refs_0_), channel_id=1, source_target_pairs={{0,1},{1,0},{2,3},{3,2},{4,5},{5,4},{6,7},{7,6},{8,9},{9,8},{10,11... | collective-permute-start | bytes 1572872 | tf_op jit(solution)/shard_map/ppermute | solution.py:203
  12.7 5.9 %collective-permute-start.6 = (bf16[8,64,128]{2,1,0:T(8,128)(2,1)S(1)}, bf16[8,64,128]{2,1,0:T(8,128)(2,1)S(1)}, u32[]{:S(2)}, u32[]{:S(2)}) collective-permute-start(bf16[8,64,128]{2,1,0:T(8,128)(2,1)S(1)} %collective-permute-done.2.refs_3_), channel_id=1, source_target_pairs={{0,2},{1,3},{2,0},{3,1},{4,6},{5,7},{6,4},{7,5},{8,10},{9,11},{10,... | collective-permute-start | bytes 393224 | tf_op jit(solution)/shard_map/ppermute | solution.py:203
  14.3 6.0 %collective-permute-start.5 = (bf16[8,64,128]{2,1,0:T(8,128)(2,1)S(1)}, bf16[8,64,128]{2,1,0:T(8,128)(2,1)S(1)}, u32[]{:S(2)}, u32[]{:S(2)}) collective-permute-start(bf16[8,64,128]{2,1,0:T(8,128)(2,1)S(1)} %collective-permute-done.2.refs_3_), channel_id=1, source_target_pairs={{0,4},{1,5},{2,6},{3,7},{4,0},{5,1},{6,2},{7,3},{8,12},{9,13},{10,... | collective-permute-start | bytes 393224 | tf_op jit(solution)/shard_map/ppermute | solution.py:203
  16.0 8.9 %collective-permute-start.4 = (bf16[8,64,128]{2,1,0:T(8,128)(2,1)S(1)}, bf16[8,64,128]{2,1,0:T(8,128)(2,1)S(1)}, u32[]{:S(2)}, u32[]{:S(2)}) collective-permute-start(bf16[8,64,128]{2,1,0:T(8,128)(2,1)S(1)} %collective-permute-done.refs_1_), channel_id=1, source_target_pairs={{0,8},{1,9},{2,10},{3,11},{4,12},{5,13},{6,14},{7,15},{8,0},{9,1},... | collective-permute-start | bytes 393224 | tf_op jit(solution)/shard_map/ppermute | solution.py:203
  24.9 10.1 %collective-permute-start.8 = (bf16[24,64,128]{2,1,0:T(8,128)(2,1)S(1)}, bf16[24,64,128]{2,1,0:T(8,128)(2,1)S(1)}, u32[]{:S(2)}, u32[]{:S(2)}) collective-permute-start(bf16[24,64,128]{2,1,0:T(8,128)(2,1)S(1)} %shard_map.77.refs_2_), channel_id=1, source_target_pairs={{0,1},{1,0},{2,3},{3,2},{4,5},{5,4},{6,7},{7,6},{8,9},{9,8},{10,11... | collective-permute-start | bytes 1179656 | tf_op jit(solution)/shard_map/ppermute | solution.py:203
  25.0 5.9 %collective-permute-start.7 = (bf16[8,64,128]{2,1,0:T(8,128)(2,1)S(1)}, bf16[8,64,128]{2,1,0:T(8,128)(2,1)S(1)}, u32[]{:S(2)}, u32[]{:S(2)}) collective-permute-start(bf16[8,64,128]{2,1,0:T(8,128)(2,1)S(1)} %collective-permute-done.1.refs_2_), channel_id=1, source_target_pairs={{0,2},{1,3},{2,0},{3,1},{4,6},{5,7},{6,4},{7,5},{8,10},{9,11},{10,... | collective-permute-start | bytes 393224 | tf_op jit(solution)/shard_map/ppermute | solution.py:203
  30.9 4.1 %collective-permute-start.9 = (bf16[8,64,128]{2,1,0:T(8,128)(2,1)S(1)}, bf16[8,64,128]{2,1,0:T(8,128)(2,1)S(1)}, u32[]{:S(2)}, u32[]{:S(2)}) collective-permute-start(bf16[8,64,128]{2,1,0:T(8,128)(2,1)S(1)} %collective-permute-done.7.refs_3_), channel_id=1, source_target_pairs={{0,1},{1,0},{2,3},{3,2},{4,5},{5,4},{6,7},{7,6},{8,9},{9,8},{10,11... | collective-permute-start | bytes 393224 | tf_op jit(solution)/shard_map/ppermute | solution.py:203
  35.7 8.1 %collective-permute-start.10 = (bf16[14,64,128]{2,1,0:T(8,128)(2,1)S(1)}, bf16[14,64,128]{2,1,0:T(8,128)(2,1)S(1)}, u32[]{:S(2)}, u32[]{:S(2)}) collective-permute-start(bf16[14,64,128]{2,1,0:T(8,128)(2,1)S(1)} %bitcast.7), channel_id=1, source_target_pairs={{0,16},{16,0},{1,17},{17,1},{2,18},{18,2},{3,19},{19,3},{4,20},{20... | collective-permute-start | bytes 688136 | tf_op jit(solution)/shard_map/ppermute | solution.py:267
